TPU v7x, 32 devices: a whole 2x2x4 slice. The times are simulated.
32 devices in a mesh: dp: 8 (over y, x, core), tensor: 4 (over z).
Axes of the slice: x: 2, y: 2, z: 4, core: 2. Of those that a mesh axis runs over, the one named last changes fastest.
Arguments:
- tokens: bfloat16 [16384, 768], P(('dp', 'tensor')), may hold values from -6 to 6
- page_lengths: int32 [32], P('dp'), may hold values from 64 to 512, as said below
- w_query: bfloat16 [768, 768], P(None, 'tensor'), may hold values from -0.21875 to 0.21875
- b_query: bfloat16 [768], P('tensor'), may hold values from -1.796875 to 1.796875
- w_key: bfloat16 [768, 768], P(None, 'tensor'), may hold values from -0.21875 to 0.21875
- w_value: bfloat16 [768, 768], P(None, 'tensor'), may hold values from -0.21875 to 0.21875
- b_value: bfloat16 [768], P('tensor'), may hold values from -1.796875 to 1.796875
- w_out: bfloat16 [768, 768], P('tensor'), may hold values from -3.5 to 3.5
- b_out: bfloat16 [768], replicated, may hold values from -1.796875 to 1.796875
- ln1_gain: bfloat16 [768], replicated, may hold values from 0.099609375 to 1.8984375
- ln1_bias: bfloat16 [768], replicated, may hold values from -1.796875 to 1.796875
- w_up: bfloat16 [768, 3072], P(None, 'tensor'), may hold values from -0.21875 to 0.21875
- b_up: bfloat16 [3072], P('tensor'), may hold values from -3 to 3
- w_down: bfloat16 [3072, 768], P('tensor'), may hold values from -0.109375 to 0.109375
- b_down: bfloat16 [768], replicated, may hold values from -1.796875 to 1.796875
- ln2_gain: bfloat16 [768], replicated, may hold values from 0.099609375 to 1.8984375
- ln2_bias: bfloat16 [768], replicated, may hold values from -1.796875 to 1.796875
- cotangent: bfloat16 [16384, 768], P(('dp', 'tensor')), may hold values from -6 to 6
Outputs:
- output: bfloat16 [16384, 768], P(('dp', 'tensor'))
- grad_tokens: bfloat16 [16384, 768], P(('dp', 'tensor'))
- grad_w_query: float32 [768, 768], P(None, 'tensor')
- grad_b_query: float32 [768], P('tensor')
- grad_w_key: float32 [768, 768], P(None, 'tensor')
- grad_w_value: float32 [768, 768], P(None, 'tensor')
- grad_b_value: float32 [768], P('tensor')
- grad_w_out: float32 [768, 768], P('tensor')
- grad_b_out: float32 [768], replicated
- grad_ln1_gain: float32 [768], replicated
- grad_ln1_bias: float32 [768], replicated
- grad_w_up: float32 [768, 3072], P(None, 'tensor')
- grad_b_up: float32 [3072], P('tensor')
- grad_w_down: float32 [3072, 768], P('tensor')
- grad_b_down: float32 [768], replicated
- grad_ln2_gain: float32 [768], replicated
- grad_ln2_bias: float32 [768], replicated
Inputs may be any that keep to these rules, and one draw needn't show every extreme that they name: `page_lengths`: the number of real tokens of page p; the keys of a page at positions from its length on are padding.
All inputs are finite; a program needn't handle non-finite values.
Results may differ from a plain program's by a relative error of at most 0.023.
Values may be sent and summed in bfloat16 or wider, within the bound.
No kernel may reach another device: no remote copies, remote signals or barrier semaphores. Data moves between devices by JAX's collectives and lax.ppermute only.
A program may use at most 128 MiB of HBM per device.

v0:
```python
from functools import partial

import jax
import jax.numpy as jnp
from jax import lax
from jax.sharding import PartitionSpec as P

HD = 64
SEQ = 512


epsilon = 1e-12
masked_score = -1000000000.0


def row_dot(matrix_a, matrix_b):
    return jnp.dot(matrix_a, matrix_b, preferred_element_type=jnp.float32)


def inner_rows(matrix_a, matrix_b):
    return lax.dot_general(
        matrix_a, matrix_b, (((0,), (0,)), ((), ())), preferred_element_type=jnp.float32
    )


def outer_cols(matrix_a, matrix_b):
    return lax.dot_general(
        matrix_a, matrix_b, (((1,), (1,)), ((), ())), preferred_element_type=jnp.float32
    )


def norm_forward(values, gain, shift):
    centred = values - jnp.mean(values, axis=-1, keepdims=True)
    variance = jnp.mean(centred * centred, axis=-1, keepdims=True)
    inverse = lax.rsqrt(variance + epsilon)
    normal = centred * inverse
    return (normal * gain + shift, normal, inverse)


def norm_backward(grad_out, gain, normal, inverse):
    scaled = grad_out * gain
    return inverse * (
        scaled
        - jnp.mean(scaled, axis=-1, keepdims=True)
        - normal * jnp.mean(scaled * normal, axis=-1, keepdims=True)
    )


def page_scores(queries, key_rows, length, local_heads):
    head_split = (SEQ, local_heads, HD)
    scores = jnp.einsum(
        "qhd,khd->hqk",
        queries.reshape(head_split),
        key_rows.reshape(head_split),
        preferred_element_type=jnp.float32,
    ) * HD ** (-0.5)
    key_mask = jnp.arange(SEQ) < length
    return jnp.where(key_mask[None, None, :], scores, masked_score)


def page_forward(queries, key_rows, values, length, local_heads):
    scores = page_scores(queries, key_rows, length, local_heads)
    row_top = jnp.max(scores, axis=-1, keepdims=True)
    log_norm = row_top + jnp.log(jnp.sum(jnp.exp(scores - row_top), axis=-1, keepdims=True))
    attn_probs = jnp.exp(scores - log_norm).astype(jnp.bfloat16)
    context = jnp.einsum(
        "hqk,khd->qhd",
        attn_probs,
        values.reshape(SEQ, local_heads, HD),
        preferred_element_type=jnp.float32,
    )
    return (context.reshape(SEQ, local_heads * HD).astype(jnp.bfloat16), log_norm)


def page_backward(queries, key_rows, values, grad_context, log_norm, length, local_heads):
    head_split = (SEQ, local_heads, HD)
    local_width = local_heads * HD
    scores = page_scores(queries, key_rows, length, local_heads)
    attn_probs = jnp.exp(scores - log_norm)
    grad_heads = grad_context.reshape(head_split)
    grad_values = jnp.einsum(
        "hqk,qhd->khd",
        attn_probs.astype(jnp.bfloat16),
        grad_heads,
        preferred_element_type=jnp.float32,
    )
    grad_probs = jnp.einsum(
        "qhd,khd->hqk", grad_heads, values.reshape(head_split), preferred_element_type=jnp.float32
    )
    grad_scores = (
        attn_probs * (grad_probs - jnp.sum(attn_probs * grad_probs, axis=-1, keepdims=True))
    ).astype(jnp.bfloat16)
    score_scale = HD ** (-0.5)
    grad_queries = (
        jnp.einsum(
            "hqk,khd->qhd",
            grad_scores,
            key_rows.reshape(head_split),
            preferred_element_type=jnp.float32,
        )
        * score_scale
    )
    grad_keys = (
        jnp.einsum(
            "hqk,qhd->khd",
            grad_scores,
            queries.reshape(head_split),
            preferred_element_type=jnp.float32,
        )
        * score_scale
    )
    return jnp.concatenate(
        [
            grad_queries.reshape(SEQ, local_width).astype(jnp.bfloat16),
            grad_keys.reshape(SEQ, local_width).astype(jnp.bfloat16),
            grad_values.reshape(SEQ, local_width).astype(jnp.bfloat16),
        ],
        axis=1,
    )


def attention_all(queries, key_rows, values, lengths, local_heads):
    page_count = lengths.shape[0]
    local_width = local_heads * HD

    def by_pages(array_in):
        return array_in.reshape(page_count, SEQ, array_in.shape[1])

    def attend(page_item):
        return page_forward(page_item[0], page_item[1], page_item[2], page_item[3], local_heads)

    context, log_norm = lax.map(
        attend, (by_pages(queries), by_pages(key_rows), by_pages(values), lengths)
    )
    return (context.reshape(page_count * SEQ, local_width), log_norm)


def attention_back_all(queries, key_rows, values, grad_context, log_norm, lengths, local_heads):
    page_count = lengths.shape[0]
    local_width = local_heads * HD

    def by_pages(array_in):
        return array_in.reshape(page_count, SEQ, array_in.shape[1])

    def attend_back(page_item):
        return page_backward(
            page_item[0],
            page_item[1],
            page_item[2],
            page_item[3],
            page_item[4],
            page_item[5],
            local_heads,
        )

    grad_joint = lax.map(
        attend_back,
        (
            by_pages(queries),
            by_pages(key_rows),
            by_pages(values),
            by_pages(grad_context),
            log_norm,
            lengths,
        ),
    )
    return grad_joint.reshape(page_count * SEQ, 3 * local_width)


def project_joint(rows_in, w_joint, b_query, b_value, local_width):
    projected = row_dot(rows_in, w_joint)
    queries = (projected[:, :local_width] + b_query.astype(jnp.float32)).astype(jnp.bfloat16)
    key_rows = projected[:, local_width : 2 * local_width].astype(jnp.bfloat16)
    values = (projected[:, 2 * local_width :] + b_value.astype(jnp.float32)).astype(jnp.bfloat16)
    return (queries, key_rows, values)


def joint_grads(rows_in, grad_joint, local_width):
    grad_w_joint = inner_rows(rows_in, grad_joint)
    joint_sums = jnp.sum(grad_joint.astype(jnp.float32), axis=0)
    return (
        grad_w_joint[:, :local_width],
        joint_sums[:local_width],
        grad_w_joint[:, local_width : 2 * local_width],
        grad_w_joint[:, 2 * local_width :],
        joint_sums[2 * local_width :],
    )


def split_heads(
    tokens,
    page_lengths,
    w_query,
    b_query,
    w_key,
    w_value,
    b_value,
    w_out,
    b_out,
    ln1_gain,
    ln1_bias,
    w_up,
    b_up,
    w_down,
    b_down,
    ln2_gain,
    ln2_bias,
    cotangent,
):
    share_rows = tokens.shape[0]
    local_width = w_query.shape[1]
    local_heads = local_width // HD
    w_joint = jnp.concatenate([w_query, w_key, w_value], axis=1)
    all_tokens = lax.all_gather(tokens, "tensor", axis=0, tiled=True)
    queries, key_rows, values = project_joint(all_tokens, w_joint, b_query, b_value, local_width)
    context, log_norm = attention_all(queries, key_rows, values, page_lengths, local_heads)
    attended = lax.psum_scatter(
        row_dot(context, w_out).astype(jnp.bfloat16), "tensor", scatter_dimension=0, tiled=True
    ).astype(jnp.float32)
    gain_one = ln1_gain.astype(jnp.float32)
    normed, normal_one, inverse_one = norm_forward(
        tokens.astype(jnp.float32) + attended + b_out.astype(jnp.float32),
        gain_one,
        ln1_bias.astype(jnp.float32),
    )
    all_normed = lax.all_gather(normed.astype(jnp.bfloat16), "tensor", axis=0, tiled=True)
    preact = row_dot(all_normed, w_up) + b_up.astype(jnp.float32)
    gelu_value, gelu_back = jax.vjp(partial(jax.nn.gelu, approximate=False), preact)
    activated = gelu_value.astype(jnp.bfloat16)
    branch = lax.psum_scatter(
        row_dot(
            lax.slice_in_dim(activated, 0, share_rows * lax.axis_size("tensor"), axis=0), w_down
        ).astype(jnp.bfloat16),
        "tensor",
        scatter_dimension=0,
        tiled=True,
    ).astype(jnp.float32)
    gain_two = ln2_gain.astype(jnp.float32)
    output_value, normal_two, inverse_two = norm_forward(
        normed + branch + b_down.astype(jnp.float32), gain_two, ln2_bias.astype(jnp.float32)
    )
    grad_out = cotangent.astype(jnp.float32)
    grad_gain_two = jnp.sum(grad_out * normal_two, axis=0)
    grad_bias_two = jnp.sum(grad_out, axis=0)
    grad_branch = norm_backward(grad_out, gain_two, normal_two, inverse_two)
    grad_b_down = jnp.sum(grad_branch, axis=0)
    shard_rows = lax.all_gather(grad_branch.astype(jnp.bfloat16), "tensor", axis=0, tiled=True)
    offset = jnp.int32(0)
    weight_total = jnp.zeros(w_down.shape, jnp.float32)
    grad_act = jnp.zeros(preact.shape, jnp.float32)
    act_rows = lax.dynamic_slice_in_dim(activated, offset, shard_rows.shape[0], 0)
    weight_total = weight_total + inner_rows(act_rows, shard_rows)
    grad_act = lax.dynamic_update_slice_in_dim(grad_act, outer_cols(shard_rows, w_down), offset, 0)
    grad_w_down, grad_act = (weight_total, grad_act)
    grad_preact = gelu_back(grad_act)[0].astype(jnp.bfloat16)
    grad_w_up = inner_rows(all_normed, grad_preact)
    grad_b_up = jnp.sum(grad_preact.astype(jnp.float32), axis=0)
    ffn_grads = (grad_w_up, grad_b_up, grad_w_down)
    grad_normed = grad_branch + lax.psum_scatter(
        outer_cols(grad_preact, w_up).astype(jnp.bfloat16),
        "tensor",
        scatter_dimension=0,
        tiled=True,
    ).astype(jnp.float32)
    grad_gain_one = jnp.sum(grad_normed * normal_one, axis=0)
    grad_bias_one = jnp.sum(grad_normed, axis=0)
    grad_residual = norm_backward(grad_normed, gain_one, normal_one, inverse_one)
    grad_b_out = jnp.sum(grad_residual, axis=0)
    shard_rows = lax.all_gather(grad_residual.astype(jnp.bfloat16), "tensor", axis=0, tiled=True)
    offset = jnp.int32(0)
    weight_total = jnp.zeros(w_out.shape, jnp.float32)
    grad_context = jnp.zeros(context.shape, jnp.float32)
    context_rows = lax.dynamic_slice_in_dim(context, offset, shard_rows.shape[0], 0)
    weight_total = weight_total + inner_rows(context_rows, shard_rows)
    grad_context = lax.dynamic_update_slice_in_dim(
        grad_context, outer_cols(shard_rows, w_out), offset, 0
    )
    grad_w_out, grad_context = (weight_total, grad_context)
    grad_context = grad_context.astype(jnp.bfloat16)
    grad_joint = attention_back_all(
        queries, key_rows, values, grad_context, log_norm, page_lengths, local_heads
    )
    grad_w_query, grad_b_query, grad_w_key, grad_w_value, grad_b_value = joint_grads(
        all_tokens, grad_joint, local_width
    )
    grad_tokens = (
        grad_residual
        + lax.psum_scatter(
            outer_cols(grad_joint, w_joint).astype(jnp.bfloat16),
            "tensor",
            scatter_dimension=0,
            tiled=True,
        ).astype(jnp.float32)
    ).astype(jnp.bfloat16)
    attn_grads = (grad_w_query, grad_b_query, grad_w_key, grad_w_value, grad_b_value, grad_w_out)
    small_grads = (
        grad_gain_one,
        grad_bias_one,
        grad_b_out,
        grad_gain_two,
        grad_bias_two,
        grad_b_down,
    )
    return (
        output_value.astype(jnp.bfloat16),
        grad_tokens,
        attn_grads,
        ffn_grads,
        small_grads,
        None,
    )


def per_device(
    tokens,
    page_lengths,
    w_query,
    b_query,
    w_key,
    w_value,
    b_value,
    w_out,
    b_out,
    ln1_gain,
    ln1_bias,
    w_up,
    b_up,
    w_down,
    b_down,
    ln2_gain,
    ln2_bias,
    cotangent,
):
    arguments = (
        tokens,
        page_lengths,
        w_query,
        b_query,
        w_key,
        w_value,
        b_value,
        w_out,
        b_out,
        ln1_gain,
        ln1_bias,
        w_up,
        b_up,
        w_down,
        b_down,
        ln2_gain,
        ln2_bias,
        cotangent,
    )
    output_value, grad_tokens, attn_grads, ffn_grads, small_grads, ffn_sums = split_heads(
        *arguments
    )
    summed = lax.psum(attn_grads + ffn_grads, "dp")
    small_sums = lax.psum(
        (
            small_grads[0],
            small_grads[1],
            small_grads[2],
            small_grads[3],
            small_grads[4],
            small_grads[5],
        ),
        ("dp", "tensor"),
    )
    return (
        output_value,
        grad_tokens,
        summed[0],
        summed[1],
        summed[2],
        summed[3],
        summed[4],
        summed[5],
        small_sums[2],
        small_sums[0],
        small_sums[1],
        summed[6],
        summed[7],
        summed[8],
        small_sums[5],
        small_sums[3],
        small_sums[4],
    )


def solution(mesh):
    return jax.shard_map(
        per_device,
        mesh=mesh,
        in_specs=(
            P(("dp", "tensor"), None),
            P("dp"),
            P(None, "tensor"),
            P("tensor"),
            P(None, "tensor"),
            P(None, "tensor"),
            P("tensor"),
            P("tensor", None),
            P(),
            P(),
            P(),
            P(None, "tensor"),
            P("tensor"),
            P("tensor", None),
            P(),
            P(),
            P(),
            P(("dp", "tensor"), None),
        ),
        out_specs=(
            P(("dp", "tensor"), None),
            P(("dp", "tensor"), None),
            P(None, "tensor"),
            P("tensor"),
            P(None, "tensor"),
            P(None, "tensor"),
            P("tensor"),
            P("tensor", None),
            P(),
            P(),
            P(),
            P(None, "tensor"),
            P("tensor"),
            P("tensor", None),
            P(),
            P(),
            P(),
        ),
        check_vma=False,
    )
```

profile of v0, /device:TPU:0, one launch (start us, length us, event | category | flops | bytes accessed | tf_op | source)
XLA Modules:
  0.0 776.0 jit_solution(8141376067380664361)
XLA Ops:
  9.3 1.0 constant_dynamic-update-slice_fusion.3
  10.3 1.0 constant_dynamic-update-slice_fusion.2
  11.3 1.0 constant_dynamic-update-slice_fusion.1
  12.3 63.6 %all-gather.5.cloned.1.call-done = bf16[2048,768]{1,0:T(8,128)(2,1)} async-done(((bf16[512,768]{1,0:T(8,128)(2,1)}), bf16[2048,768]{1,0:T(8,128)(2,1)}) %all-gather.5.cloned.1.call-update) | async-done | bytes 3145744 | tf_op jit(solution)/shard_map/all_gather | solution.py:214
  75.8 3.9 convolution_bitcast_fusion
  80.8 19.8 %while.22 = (s32[]{:T(128)}, bf16[4,512,192]{1,2,0:T(8,128)(2,1)}, f32[4,3,512,1]{2,1,3,0:T(4,128)}, bf16[4,512,192]{1,2,0:T(8,128)(2,1)S(1)}, s32[4]{0:T(128)S(...) while((s32[]{:T(128)}, bf16[4,512,192]{1,2,0:T(8,128)(2,1)}, ...), condition=%wide.region_3.4_spmd, body=%wide.region_0.3_spmd.sunk | while | flops 210074624 | bytes 11850861 | solution.py:132
  101.4 1.2 copy.67
  102.7 3.6 convolution_convert_fusion.3
  107.6 57.8 %reduce-scatter.5.cloned.1.call-done = bf16[512,768]{1,0:T(8,128)(2,1)} async-done(((bf16[2048,768]{1,0:T(8,128)(2,1)}), bf16[512,768]{1,0:T(8,128)(2,1)}) %reduce-scatter.5.cloned.1.call-update) | async-done | bytes 786448 | tf_op jit(solution)/shard_map/reduce_scatter | solution.py:217
  165.4 1.5 fusion.30
  167.0 1.6 multiply_reduce_fusion.4
  168.6 1.3 fusion.29
  170.5 1.3 convert_element_type.158
  171.8 61.8 %all-gather.7.cloned.1.call-done = bf16[2048,768]{1,0:T(8,128)(2,1)} async-done(((bf16[512,768]{1,0:T(8,128)(2,1)}), bf16[2048,768]{1,0:T(8,128)(2,1)}) %all-gather.7.cloned.1.call-update) | async-done | bytes 3145744 | tf_op jit(solution)/shard_map/all_gather | solution.py:226
  233.6 18.4 %multiply_convert_fusion.1 = (bf16[2048,768]{1,0:T(8,128)(2,1)S(1)}, f32[2048,768]{1,0:T(8,128)}, f32[2048,768]{1,0:T(8,128)}) fusion(f32[768]{0:T(1024)} %convert_element_type.158, bf16[2048,768]{1,0:T(8,128)(2,1)} %all-gather.7.cloned.1.call-done, bf16[768,768]{1,0:T(8,128)(2,1)S(1)} %copy-done), kind=kOutput, calls=%fused_computation.38 | convolution fusion | flops 2519728128 | bytes 20057088 | tf_op jit(solution)/shard_map/dot_general | solution.py:17
  252.0 1.7 copy-done.38
  253.7 4.0 convolution_convert_fusion.1
  257.8 1.3 convert_element_type.162
  259.0 1.3 convert_element_type.163
  260.3 1.3 convert_element_type.164
  261.6 55.2 %reduce-scatter.7.cloned.1.call-done = bf16[512,768]{1,0:T(8,128)(2,1)} async-done(((bf16[2048,768]{1,0:T(8,128)(2,1)}), bf16[512,768]{1,0:T(8,128)(2,1)}) %reduce-scatter.7.cloned.1.call-update) | async-done | bytes 786448 | tf_op jit(solution)/shard_map/reduce_scatter | solution.py:230
  316.8 2.0 fusion.35
  319.1 1.3 fusion.26
  320.4 2.3 fusion.33
  323.0 63.5 %all-gather.9.cloned.1.call-done = bf16[2048,768]{1,0:T(8,128)(2,1)} async-done(((bf16[512,768]{1,0:T(8,128)(2,1)}), bf16[2048,768]{1,0:T(8,128)(2,1)}) %all-gather.9.cloned.1.call-update) | async-done | bytes 3145744 | tf_op jit(solution)/shard_map/all_gather | solution.py:247
  386.5 11.0 %convert_reduce_fusion = (f32[768]{0:T(1024)}, bf16[2048,768]{1,0:T(8,128)(2,1)S(1)}) fusion(f32[2048,768]{1,0:T(8,128)} %get-tuple-element.195, f32[2048,768]{1,0:T(8,128)} %get-tuple-element.214, f32[768]{0:T(1024)} %convert_element_type.158, bf16[2048,768]{1,0:T(8,128)(2,1)} %all-gather.9.cloned.1.call-done, bf16[768,768]{1,0:T(8,128)(2,1)} %param.35), kind=kOutput, calls=%fused_computation.36 | convolution fusion | flops 2442657024 | bytes 20060160 | tf_op jit(solution)/shard_map/dot_general | solution.py:27
  397.5 1.7 copy-done.39
  399.1 4.0 convolution_convert_fusion
  403.2 59.0 %reduce-scatter.9.cloned.1.call-done = bf16[512,768]{1,0:T(8,128)(2,1)} async-done(((bf16[2048,768]{1,0:T(8,128)(2,1)}), bf16[512,768]{1,0:T(8,128)(2,1)}) %reduce-scatter.9.cloned.1.call-update) | async-done | bytes 786448 | tf_op jit(solution)/shard_map/reduce_scatter | solution.py:259
  462.2 3.3 multiply_reduce_fusion.1
  465.6 2.8 fusion.32
  468.4 1.2 copy-done.4
  469.6 1.0 convert_element_type.171
  470.8 63.4 %all-gather.11.cloned.1.call-done = bf16[2048,768]{1,0:T(8,128)(2,1)} async-done(((bf16[512,768]{1,0:T(8,128)(2,1)}), bf16[2048,768]{1,0:T(8,128)(2,1)}) %all-gather.11.cloned.1.call-update) | async-done | bytes 3145744 | tf_op jit(solution)/shard_map/all_gather | solution.py:269
  534.2 3.1 convolution_convert_fusion.4
  537.4 36.0 %while.23 = (s32[]{:T(128)}, bf16[4,512,576]{1,2,0:T(8,128)(2,1)}, bf16[4,512,192]{1,2,0:T(8,128)(2,1)}, s32[4]{0:T(128)S(1)}, bf16[4,512,192]{1,2,0:T(8,128)(2,...) while((s32[]{:T(128)}, bf16[4,512,576]{1,2,0:T(8,128)(2,1)}, ...), condition=%wide.region_17.18_spmd, body=%wide.region_15.17_spmd.sunk | while | flops 512654336 | bytes 28343928 | solution.py:156
  537.4 1.0 constant_dynamic-slice_fusion.13
  539.0 1.1 constant_dynamic-slice_fusion.14
  542.0 1.1 multiply_reduce_fusion.7
  548.0 1.1 constant_dynamic-slice_fusion.14
  551.0 1.1 multiply_reduce_fusion.7
  556.9 1.1 constant_dynamic-slice_fusion.14
  559.9 1.1 multiply_reduce_fusion.7
  565.9 1.1 constant_dynamic-slice_fusion.14
  568.9 1.1 multiply_reduce_fusion.7
  573.4 2.0 copy.68
  575.4 1.4 copy-done.14
  576.8 4.0 convolution_convert_fusion.2
  581.2 7.0 fusion.42
  588.3 4.2 fusion.41
  592.5 2.0 convolution_bitcast_fusion.1
  594.5 1.2 fusion.37
  595.7 1.3 copy-done.9
  597.0 1.6 fusion.40
  599.4 45.2 %all-reduce = (f32[768]{0:T(1024)}, f32[768]{0:T(1024)}, f32[768]{0:T(1024)}, f32[768]{0:T(1024)}, f32[768]{0:T(1024)}, /*index=5*/f32[768]{0:T(1024)}) all-reduce(f32[768]{0:T(1024)S(1)} %copy-done.27, f32[768]{0:T(1024)S(1)} %copy-done.24, f32[768]{0:T(1024)S(1)} %copy-done.25, ...), channel_id=1, replica_groups=mesh['dp'=8,'tensor'=4] {'dp','tensor'}, use_global_device_ids=true, to_apply=%region_27.28 | all-reduce | flops 4608 | bytes 36864 | tf_op jit(solution)/shard_map/psum | solution.py:358
  644.6 2.1 convert_reduce_fusion.1
  646.7 14.4 %all-reduce.1 = (f32[192]{0:T(256)}, f32[192]{0:T(256)}, f32[768]{0:T(1024)}) all-reduce(f32[192]{0:T(256)S(1)} %get-tuple-element.213, f32[192]{0:T(256)S(1)} %get-tuple-element.212, f32[768]{0:T(1024)S(1)} %copy-done.29), channel_id=1, replica_groups=mesh['dp'=8,'tensor'=4] {'dp'}, use_global_device_ids=true, to_apply=%region_21.22 | all-reduce | flops 1152 | bytes 9216 | tf_op jit(solution)/shard_map/psum | solution.py:357
  661.2 2.2 add_convert_fusion.1
  663.3 96.4 %all-reduce.5.cloned.1.call-done = (f32[768,192]{0,1:T(8,128)}, f32[768,192]{0,1:T(8,128)}, f32[768,192]{0,1:T(8,128)}, f32[192,768]{1,0:T(8,128)}, f32[768,768]{1,0:T(8,128)}, /*index=5*/f32[768,768]{1,0:T(8,128)}) async-done(((f32[768,192]{0,1:T(8,128)}, f32[768,192]{0,1:T(8,128)}, f32[768,192]{0,1:T(8,128)}, f32[192,768]{1,0:T(8,128)}, f32[768,768]{1,0:T(8,128)}, /*index=5*/f32[768,768]{1,0:T(8,128)}), ...) | async-done | bytes 7077904 | tf_op jit(solution)/shard_map/psum | solution.py:357
  759.7 2.1 copy.103
  761.8 1.9 copy.104
  763.7 1.9 copy.105
  766.4 1.4 copy.107
  767.8 1.4 copy.108
  (195 shorter events, 54.6 us)
Async XLA Ops:
  7.2 226.4 %copy-start = (bf16[768,768]{1,0:T(8,128)(2,1)S(1)}, bf16[768,768]{1,0:T(8,128)(2,1)}, u32[]{:S(2)}) copy-start(bf16[768,768]{1,0:T(8,128)(2,1)} %param.33) | copy-start | bytes 3538948
  7.2 68.6 %all-gather.5.cloned.1.call-start = ((), (), s32[]{:S(2)}) async-start(), calls=%async_computation.4 | async-start | bytes 3932160 | tf_op jit(solution)/shard_map/all_gather | solution.py:214
  7.9 157.5 %reduce-scatter.5.cloned.1.call-start = ((), (), s32[]{:S(2)}) async-start(), calls=%async_computation.5 | async-start | bytes 3932160 | tf_op jit(solution)/shard_map/reduce_scatter | solution.py:217
  12.3 67.5 %copy-start.18 = (bf16[768,576]{0,1:T(8,128)(2,1)}, bf16[768,576]{0,1:T(8,128)(2,1)S(1)}, u32[]{:S(2)}) copy-start(bf16[768,576]{0,1:T(8,128)(2,1)S(1)} %constant_dynamic-update-slice_fusion.1) | copy-start | bytes 2654212
  80.1 0.7 copy-start.36
  100.5 0.9 copy-start.8
  100.6 2.1 copy-start.6
  100.6 5.7 copy-start.7
  106.3 0.7 copy-start.30
  106.3 0.7 copy-start.31
  106.3 0.7 copy-start.32
  106.3 59.1 %copy-start.2 = (bf16[512,768]{1,0:T(8,128)(2,1)S(1)}, bf16[512,768]{1,0:T(8,128)(2,1)}, u32[]{:S(2)}) copy-start(bf16[512,768]{1,0:T(8,128)(2,1)} %param.22) | copy-start | bytes 2359300
  106.3 127.3 %all-gather.7.cloned.1.call-start = ((), (), s32[]{:S(2)}) async-start(), calls=%async_computation.6 | async-start | bytes 3932160 | tf_op jit(solution)/shard_map/all_gather | solution.py:226
  165.4 3.1 copy-start.3
  165.4 3.1 copy-start.20
  169.9 146.8 %reduce-scatter.7.cloned.1.call-start = ((), (), s32[]{:S(2)}) async-start(), calls=%async_computation.7 | async-start | bytes 3932160 | tf_op jit(solution)/shard_map/reduce_scatter | solution.py:230
  233.6 20.1 %copy-start.35 = (bf16[768,768]{1,0:T(8,128)(2,1)S(1)}, bf16[768,768]{1,0:T(8,128)(2,1)}, u32[]{:S(2)}) copy-start(bf16[768,768]{1,0:T(8,128)(2,1)} %param.35) | copy-start | bytes 3538948
  252.0 1.7 copy-start.38
  257.7 128.7 %all-gather.9.cloned.1.call-start = ((), (), s32[]{:S(2)}) async-start(), calls=%async_computation.8 | async-start | bytes 3932160 | tf_op jit(solution)/shard_map/all_gather | solution.py:247
  316.8 2.3 copy-start.11
  316.8 2.3 copy-start.21
  316.8 3.7 copy-start.28
  322.8 139.5 %reduce-scatter.9.cloned.1.call-start = ((), (), s32[]{:S(2)}) async-start(), calls=%async_computation.9 | async-start | bytes 3932160 | tf_op jit(solution)/shard_map/reduce_scatter | solution.py:259
  397.5 1.7 copy-start.39
  403.2 131.1 %all-gather.11.cloned.1.call-start = ((), (), s32[]{:S(2)}) async-start(), calls=%async_computation.10 | async-start | bytes 3932160 | tf_op jit(solution)/shard_map/all_gather | solution.py:269
  462.2 3.3 copy-start.10
  465.6 68.7 %copy-start.17 = (bf16[192,768]{1,0:T(8,128)(2,1)S(1)}, bf16[192,768]{1,0:T(8,128)(2,1)}, u32[]{:S(2)}) copy-start(bf16[192,768]{1,0:T(8,128)(2,1)} %param.29) | copy-start | bytes 884740
  468.4 1.2 copy-start.4
  470.5 190.6 %reduce-scatter.11.cloned.1.call-start = ((), (), s32[]{:S(2)}) async-start(), calls=%async_computation.11 | async-start | bytes 3932160 | tf_op jit(solution)/shard_map/reduce_scatter | solution.py:288
  470.8 66.5 %copy-start.37 = (s32[4]{0:T(128)S(1)}, s32[4]{0:T(128)}, u32[]{:S(2)}) copy-start(s32[4]{0:T(128)} %param.23) | copy-start | bytes 52
  573.4 3.4 copy-start.19
  575.4 1.4 copy-start.14
  580.9 178.8 %all-reduce.5.cloned.1.call-start = ((), (), s32[]{:S(2)}) async-start(), calls=%async_computation.12 | async-start | bytes 14155776 | tf_op jit(solution)/shard_map/psum | solution.py:357
  581.2 7.1 copy-start.34
  581.2 7.1 copy-start.40
  588.2 4.2 copy-start.15
  588.2 4.2 copy-start.33
  594.5 2.5 copy-start.9
  598.7 0.7 copy-start.22
  598.7 0.7 copy-start.23
  598.7 0.7 copy-start.24
  598.7 0.7 copy-start.25
  598.7 0.7 copy-start.26
  598.7 0.7 copy-start.27
  598.7 48.0 %copy-start.29 = (f32[768]{0:T(1024)S(1)}, f32[768]{0:T(1024)}, u32[]{:S(2)}) copy-start(f32[768]{0:T(1024)} %get-tuple-element.188) | copy-start | bytes 9220
  598.7 62.5 %copy-start.5 = (f32[512,768]{1,0:T(8,128)S(1)}, f32[512,768]{1,0:T(8,128)}, u32[]{:S(2)}) copy-start(f32[512,768]{1,0:T(8,128)} %copy-done.4) | copy-start | bytes 4718596
  759.7 5.9 copy-start.16
  759.7 6.7 copy-start.13
  765.6 2.2 copy-start.12
  766.4 2.8 copy-start.1
Sparse Core Ops, SparseCore 0:
  9.6 66.1 all-gather.4
  106.5 58.8 reduce-scatter.4
  170.1 63.5 all-gather.6
  257.8 58.8 reduce-scatter.6
  322.9 63.5 all-gather.8
  403.3 58.8 reduce-scatter.8
  470.7 63.5 all-gather.10
  581.0 59.8 reduce-scatter.10
  645.6 114.0 all-reduce.4
where the time goes:
time: 783 us; the launch traced here: 776 us
  waiting for transfers between devices  521 us (67%)
  matrix products  86.7 us (11%)
  blocking collectives  59.7 us (8%)
  other arithmetic  46.2 us (6%)
  local copies, waits for them, and re-layouts  45.7 us (6%)
  between operations  14.5 us (2%)
    psum x1, waiting for transfers between devices, per_device(): summed = lax.psum(attn_grads + ffn_grads, 'dp')  96.4 us
    all_gather x1, waiting for transfers between devices, split_heads(): all_tokens = lax.all_gather(tokens, 'tensor', axis=0, tiled=True)  63.6 us
    all_gather x1, waiting for transfers between devices, split_heads(): lax.all_gather(grad_branch.astype(jnp.bfloat16), 'tensor', axis=0, tiled=...  63.5 us
    all_gather x1, waiting for transfers between devices, split_heads(): lax.all_gather(grad_residual.astype(jnp.bfloat16), 'tensor', axis=0, tile...  63.4 us
    all_gather x1, waiting for transfers between devices, split_heads(): lax.all_gather(normed.astype(jnp.bfloat16), 'tensor', axis=0, tiled=True)  61.8 us
    reduce_scatter x1, waiting for transfers between devices, split_heads(): lax.psum_scatter(outer_cols(grad_preact, w_up).astype(jnp.bfloat16), 'ten...  59 us
    reduce_scatter x1, waiting for transfers between devices, split_heads(): lax.psum_scatter(row_dot(context, w_out).astype(jnp.bfloat16), 'tensor',...  57.8 us
    reduce_scatter x1, waiting for transfers between devices, split_heads(): lax.psum_scatter(row_dot(lax.slice_in_dim(activated, 0, share_rows * lax....  55.2 us
  transfers between devices with their start and end apart: 9, of which 8 were waited for; matrix products, arithmetic and copies ran while one was open for 4% of the time, Pallas kernels for 0%

commit v1 on v0

v1 whole, which is shorter than its diff:
```python
from functools import partial

import jax
import jax.numpy as jnp
from jax import lax
from jax.sharding import PartitionSpec as P

HD = 64
SEQ = 512
GROUP = 8


epsilon = 1e-12
masked_score = -1000000000.0
low = jnp.bfloat16
wide = jnp.float32


def dot_of(spec, left, right):
    return jnp.einsum(spec, left, right, preferred_element_type=jnp.float32)


def norm_forward(values, gain, shift):
    centred = values - jnp.mean(values, axis=-1, keepdims=True)
    variance = jnp.mean(centred * centred, axis=-1, keepdims=True)
    inverse = lax.rsqrt(variance + epsilon)
    normal = centred * inverse
    return (normal * gain + shift, normal, inverse)


def norm_backward(grad_out, gain, normal, inverse):
    scaled = grad_out * gain
    return inverse * (
        scaled
        - jnp.mean(scaled, axis=-1, keepdims=True)
        - normal * jnp.mean(scaled * normal, axis=-1, keepdims=True)
    )


def swap(array, bit, size):
    return lax.ppermute(array, "dp", [(i, i ^ bit) for i in range(size)])


def shift(array, step, size):
    return lax.ppermute(array, "tensor", [(i, (i + step) % size) for i in range(size)])


def in_order(bit, mine, other, axis):
    return jnp.where(
        bit == 0,
        jnp.stack([mine, other], axis=axis),
        jnp.stack([other, mine], axis=axis),
    )


def gather_weights(own, extra, dp_size, parts):
    place = lax.axis_index("dp") % GROUP
    rows = own.shape[0] // GROUP
    piece = lax.dynamic_slice_in_dim(own, place * rows, rows, 0)
    if extra is not None:
        piece = jnp.concatenate([piece, extra], axis=0)
    arrived = jnp.stack([shift(piece, k, parts) for k in range(1, parts)])
    others = arrived[:, rows:]
    arrived = arrived[:, :rows]
    core, xbit, ybit = place & 1, (place >> 1) & 1, (place >> 2) & 1
    over_x = swap(arrived, 2, dp_size)
    over_y = swap(arrived, 4, dp_size)
    over_xy = swap(arrived, 6, dp_size)
    low_pair = in_order(xbit, arrived, over_x, 1)
    high_pair = in_order(xbit, over_y, over_xy, 1)
    plane = in_order(ybit, low_pair, high_pair, 1)
    mate = swap(plane, 1, dp_size)
    whole = in_order(core, plane, mate, 3)
    whole = whole.reshape(parts - 1, GROUP * rows, own.shape[1])
    return jnp.concatenate([own[None], whole], axis=0), others


def take(array, index, axis):
    return lax.dynamic_index_in_dim(array, index, axis, keepdims=False)


def reduce_shares(shares, dp_size, parts):
    place = lax.axis_index("dp") % GROUP
    core, xbit, ybit = place & 1, (place >> 1) & 1, (place >> 2) & 1
    rows, cols = shares.shape[1] // GROUP, shares.shape[2]
    split = shares.reshape(parts, 2, 2, 2, rows, cols)
    recv = swap(take(split, 1 - core, 3).astype(low), 1, dp_size)
    held = (take(split, core, 3).astype(wide) + recv.astype(wide)).astype(low)
    half = parts // 2
    first, second = held[:half], held[half:]
    recv_a = swap(take(first, 1 - xbit, 2), 2, dp_size)
    recv_b = swap(take(second, 1 - ybit, 1), 4, dp_size)
    first = (take(first, xbit, 2).astype(wide) + recv_a.astype(wide)).astype(low)
    second = (take(second, ybit, 1).astype(wide) + recv_b.astype(wide)).astype(low)
    recv_a = swap(take(first, 1 - ybit, 1), 4, dp_size)
    recv_b = swap(take(second, 1 - xbit, 1), 2, dp_size)
    first = (take(first, ybit, 1).astype(wide) + recv_a.astype(wide)).astype(low)
    second = (take(second, xbit, 1).astype(wide) + recv_b.astype(wide)).astype(low)
    held = [first[k] for k in range(half)] + [second[k] for k in range(parts - half)]
    total = held[0].astype(wide)
    for k in range(1, parts):
        total = total + shift(held[k], -k, parts).astype(wide)
    bit = GROUP
    while bit < dp_size:
        total = total + swap(total, bit, dp_size)
        bit *= 2
    total = total.astype(low)
    over_x = swap(total, 2, dp_size)
    over_y = swap(total, 4, dp_size)
    over_xy = swap(total, 6, dp_size)
    low_pair = in_order(xbit, total, over_x, 0)
    high_pair = in_order(xbit, over_y, over_xy, 0)
    plane = in_order(ybit, low_pair, high_pair, 0)
    mate = swap(plane, 1, dp_size)
    whole = in_order(core, plane, mate, 2)
    return whole.reshape(GROUP * rows, cols).astype(wide)


def sum_everywhere(array, dp_size, parts):
    bit = 1
    while bit < dp_size:
        array = array + swap(array, bit, dp_size)
        bit *= 2
    bit = 1
    while bit < parts:
        array = array + lax.ppermute(array, "tensor", [(i, i ^ bit) for i in range(parts)])
        bit *= 2
    return array


def per_device(
    dp_size,
    parts,
    tokens,
    page_lengths,
    w_query,
    b_query,
    w_key,
    w_value,
    b_value,
    w_out,
    b_out,
    ln1_gain,
    ln1_bias,
    w_up,
    b_up,
    w_down,
    b_down,
    ln2_gain,
    ln2_bias,
    cotangent,
):
    me = lax.axis_index("tensor")
    width = tokens.shape[1]
    local = w_query.shape[1]
    heads = local // HD
    pages = tokens.shape[0] // SEQ
    length = lax.dynamic_slice_in_dim(page_lengths, me * pages, pages, 0)
    biases = jnp.concatenate([b_query, b_value, b_up]).reshape(-1, local)
    biases = jnp.pad(biases.reshape(-1), (0, 16 * width - biases.size)).reshape(16, width)
    attn_own = jnp.concatenate([w_query.T, w_key.T, w_value.T, w_out], axis=0)
    attn_w, others = gather_weights(attn_own, biases, dp_size, parts)
    up_w, _ = gather_weights(w_up, None, dp_size, parts)
    down_w, _ = gather_weights(w_down, None, dp_size, parts)
    biases = jnp.concatenate([biases[None], others], axis=0).reshape(parts, -1)
    bias_q = biases[:, :local].astype(wide)
    bias_v = biases[:, local : 2 * local].astype(wide)
    bias_up = biases[:, 2 * local : 2 * local + width].astype(wide)

    joint_w = attn_w[:, : 3 * local]
    out_w = attn_w[:, 3 * local :]
    projected = dot_of("md,kfd->kmf", tokens, joint_w)
    head_split = (parts, pages, SEQ, heads, HD)
    queries = (projected[:, :, :local] + bias_q[:, None]).astype(low).reshape(head_split)
    key_rows = projected[:, :, local : 2 * local].astype(low).reshape(head_split)
    values = (projected[:, :, 2 * local :] + bias_v[:, None]).astype(low).reshape(head_split)
    key_mask = jnp.arange(SEQ)[None, :] < length[:, None]
    scores = dot_of("kpqhd,kpshd->kphqs", queries, key_rows) * HD ** (-0.5)
    scores = jnp.where(key_mask[None, :, None, None, :], scores, masked_score)
    row_top = jnp.max(scores, axis=-1, keepdims=True)
    log_norm = row_top + jnp.log(jnp.sum(jnp.exp(scores - row_top), axis=-1, keepdims=True))
    probs = jnp.exp(scores - log_norm)
    context = dot_of("kphqs,kpshd->kpqhd", probs.astype(low), values).astype(low)
    context = context.reshape(parts, pages * SEQ, local)
    attended = dot_of("kmf,kfd->md", context, out_w)
    gain_one = ln1_gain.astype(wide)
    normed, normal_one, inverse_one = norm_forward(
        tokens.astype(wide) + attended + b_out.astype(wide), gain_one, ln1_bias.astype(wide)
    )
    normed_low = normed.astype(low)
    preact = dot_of("md,kdf->kmf", normed_low, up_w) + bias_up[:, None]
    gelu_value, gelu_back = jax.vjp(partial(jax.nn.gelu, approximate=False), preact)
    activated = gelu_value.astype(low)
    branch = dot_of("kmf,kfd->md", activated, down_w)
    gain_two = ln2_gain.astype(wide)
    output_value, normal_two, inverse_two = norm_forward(
        normed + branch + b_down.astype(wide), gain_two, ln2_bias.astype(wide)
    )
    grad_out = cotangent.astype(wide)
    grad_gain_two = jnp.sum(grad_out * normal_two, axis=0)
    grad_bias_two = jnp.sum(grad_out, axis=0)
    grad_branch = norm_backward(grad_out, gain_two, normal_two, inverse_two)
    grad_b_down = jnp.sum(grad_branch, axis=0)
    branch_low = grad_branch.astype(low)
    grad_w_down = dot_of("kmf,md->kfd", activated, branch_low).astype(low)
    grad_act = dot_of("md,kfd->kmf", branch_low, down_w)
    grad_preact = gelu_back(grad_act)[0].astype(low)
    grad_w_up = dot_of("md,kmf->kdf", normed_low, grad_preact).astype(low)
    grad_b_up = jnp.sum(grad_preact.astype(wide), axis=1)
    grad_normed = grad_branch + dot_of("kmf,kdf->md", grad_preact, up_w)
    ffn = jnp.concatenate([grad_w_down, grad_w_up], axis=2)
    ffn_sum = reduce_shares(ffn, dp_size, parts)
    grad_gain_one = jnp.sum(grad_normed * normal_one, axis=0)
    grad_bias_one = jnp.sum(grad_normed, axis=0)
    grad_residual = norm_backward(grad_normed, gain_one, normal_one, inverse_one)
    grad_b_out = jnp.sum(grad_residual, axis=0)
    residual_low = grad_residual.astype(low)
    grad_w_out = dot_of("kmf,md->kfd", context, residual_low)
    grad_context = dot_of("md,kfd->kmf", residual_low, out_w).astype(low).reshape(head_split)

    grad_values = dot_of("kphqs,kpqhd->kpshd", probs.astype(low), grad_context).astype(low)
    grad_probs = dot_of("kpqhd,kpshd->kphqs", grad_context, values)
    grad_scores = (
        probs * (grad_probs - jnp.sum(probs * grad_probs, axis=-1, keepdims=True))
    ).astype(low)
    scale = HD ** (-0.5)
    grad_queries = (dot_of("kphqs,kpshd->kpqhd", grad_scores, key_rows) * scale).astype(low)
    grad_keys = (dot_of("kphqs,kpqhd->kpshd", grad_scores, queries) * scale).astype(low)
    flat = (parts, pages * SEQ, local)
    grad_queries, grad_keys, grad_values = (
        array.reshape(flat) for array in (grad_queries, grad_keys, grad_values)
    )
    grad_joint = jnp.concatenate([grad_queries, grad_keys, grad_values], axis=2)
    grad_w_joint = dot_of("kmf,md->kfd", grad_joint, tokens)
    attn = jnp.concatenate([grad_w_joint, grad_w_out], axis=1).astype(low)
    attn_sum = reduce_shares(attn, dp_size, parts)
    grad_tokens = (grad_residual + dot_of("kmf,kfd->md", grad_joint, joint_w)).astype(low)

    def absolute(array):
        return jnp.take(array, (me - jnp.arange(parts)) % parts, axis=0).reshape(-1)

    small = [
        grad_b_out,
        grad_gain_one,
        grad_bias_one,
        grad_b_down,
        grad_gain_two,
        grad_bias_two,
        absolute(jnp.sum(grad_queries.astype(wide), axis=1)),
        absolute(jnp.sum(grad_values.astype(wide), axis=1)),
        absolute(grad_b_up),
    ]
    sizes = [piece.shape[0] for piece in small]
    packed = jnp.concatenate(small).reshape(-1, width)
    packed = sum_everywhere(packed, dp_size, parts).reshape(-1)
    pieces = []
    start = 0
    for size in sizes:
        pieces.append(packed[start : start + size])
        start += size

    def own_part(array):
        return take(array.reshape(parts, -1), me, 0)

    return (
        output_value.astype(low),
        grad_tokens,
        attn_sum[:local].T,
        own_part(pieces[6]),
        attn_sum[local : 2 * local].T,
        attn_sum[2 * local : 3 * local].T,
        own_part(pieces[7]),
        attn_sum[3 * local :],
        pieces[0],
        pieces[1],
        pieces[2],
        ffn_sum[:, width:],
        own_part(pieces[8]),
        ffn_sum[:, :width],
        pieces[3],
        pieces[4],
        pieces[5],
    )


def solution(mesh):
    columns, rows, both = P(None, "tensor"), P("tensor", None), P(("dp", "tensor"), None)
    share = P("tensor")
    return jax.shard_map(
        partial(per_device, mesh.shape["dp"], mesh.shape["tensor"]),
        mesh=mesh,
        in_specs=(
            both,
            P("dp"),
            columns,
            share,
            columns,
            columns,
            share,
            rows,
            P(),
            P(),
            P(),
            columns,
            share,
            rows,
            P(),
            P(),
            P(),
            both,
        ),
        out_specs=(
            both,
            both,
            columns,
            share,
            columns,
            columns,
            share,
            rows,
            P(),
            P(),
            P(),
            columns,
            share,
            rows,
            P(),
            P(),
            P(),
        ),
        check_vma=False,
    )
```

time: 783 us -> 391 us (0.50)
  the two profiles are of different devices: /device:TPU:0 before, /device:TPU:13 now
where the time goes in v1:
time: 391 us; the launch traced here: 384 us
  waiting for transfers between devices  150 us (38%)
  matrix products  76 us (19%)
  local copies, waits for them, and re-layouts  54.9 us (14%)
  other arithmetic  51.2 us (13%)
  starting transfers between devices  49.5 us (13%)
    ppermute x33, waiting for transfers between devices, swap(): return lax.ppermute(array, 'dp', [(i, i ^ bit) for i in range(size)])  101 us
    dot_general x18, matrix products, dot_of(): return jnp.einsum(spec, left, right, preferred_element_type=jnp.float32)  76 us
    ppermute x15, waiting for transfers between devices, shift(): lax.ppermute(array, 'tensor', [(i, (i + step) % size) for i in range(size)])  47.5 us
    ppermute x33, starting transfers between devices, swap(): return lax.ppermute(array, 'dp', [(i, i ^ bit) for i in range(size)])  27 us
    ppermute x15, starting transfers between devices, shift(): lax.ppermute(array, 'tensor', [(i, (i + step) % size) for i in range(size)])  17 us
    concatenate x1, local copies, waits for them, and re-layouts, per_device(): ffn = jnp.concatenate([grad_w_down, grad_w_up], axis=2)  12.8 us
    unnamed x117, local copies, waits for them, and re-layouts  11.2 us
    convert_element_type x1, other arithmetic, per_device(): probs.astype(low)  9.78 us
  transfers between devices with their start and end apart: 50, of which 25 were waited for; matrix products, arithmetic and copies ran while one was open for 18% of the time, Pallas kernels for 0%

profile of v1, /device:TPU:13, one launch (start us, length us, event | category | flops | bytes accessed | tf_op | source)
XLA Modules:
  0.0 384.5 jit_solution(15006309019877992046)
XLA Ops:
  1.9 2.3 collective-permute-start.8
  4.2 2.2 collective-permute-start.7
  8.6 2.1 concatenate.430
  14.0 2.1 collective-permute-start.14
  17.6 5.1 %collective-permute-done.7 = bf16[96,768]{1,0:T(8,128)(2,1)S(1)} collective-permute-done((bf16[96,768]{1,0:T(8,128)(2,1)S(1)}, bf16[96,768]{1,0:T(8,128)(2,1)S(1)}, u32[]{:S(2)}, u32[]{:S(2)}) %collective-permute-start.7) | collective-permute-done | bytes 147488 | tf_op jit(solution)/shard_map/ppermute | solution.py:45
  22.7 3.2 collective-permute-done.16
  26.0 6.4 %collective-permute-done.15 = bf16[96,768]{1,0:T(8,128)(2,1)S(1)} collective-permute-done((bf16[96,768]{1,0:T(8,128)(2,1)S(1)}, bf16[96,768]{1,0:T(8,128)(2,1)S(1)}, u32[]{:S(2)}, u32[]{:S(2)}) %collective-permute-start.15) | collective-permute-done | bytes 147488 | tf_op jit(solution)/shard_map/ppermute | solution.py:45
  33.5 3.1 collective-permute-done.14
  36.8 3.3 collective-permute-done.2
  41.5 2.4 collective-permute-done
  45.7 11.6 %collective-permute-done.11 = bf16[3,96,768]{2,1,0:T(8,128)(2,1)S(1)} collective-permute-done((bf16[3,96,768]{2,1,0:T(8,128)(2,1)S(1)}, bf16[3,96,768]{2,1,0:T(8,128)(2,1)S(1)}, u32[]{:S(2)}, u32[]{:S(2)}) %collective-permute-start.11) | collective-permute-done | bytes 442400 | tf_op jit(solution)/shard_map/ppermute | solution.py:41
  57.6 2.3 collective-permute-start.4
  63.0 13.1 %collective-permute-done.18 = bf16[3,96,768]{2,1,0:T(8,128)(2,1)S(1)} collective-permute-done((bf16[3,96,768]{2,1,0:T(8,128)(2,1)S(1)}, bf16[3,96,768]{2,1,0:T(8,128)(2,1)S(1)}, u32[]{:S(2)}, u32[]{:S(2)}) %collective-permute-start.18) | collective-permute-done | bytes 442400 | tf_op jit(solution)/shard_map/ppermute | solution.py:41
  78.0 2.9 collective-permute-done.5
  80.8 11.9 %collective-permute-done.4 = bf16[3,96,768]{2,1,0:T(8,128)(2,1)S(1)} collective-permute-done((bf16[3,96,768]{2,1,0:T(8,128)(2,1)S(1)}, bf16[3,96,768]{2,1,0:T(8,128)(2,1)S(1)}, u32[]{:S(2)}, u32[]{:S(2)}) %collective-permute-start.4) | collective-permute-done | bytes 442400 | tf_op jit(solution)/shard_map/ppermute | solution.py:41
  96.0 2.1 copy.67
  98.7 2.1 copy.68
  102.0 1.6 copy-done.3
  103.6 2.1 convolution_bitcast_fusion
  106.7 3.0 fusion
  109.7 2.6 exponential_reduce_fusion
  112.3 2.0 copy-done
  114.3 9.8 %fusion.2 = bf16[4,3,512,512]{2,3,1,0:T(8,128)(2,1)} fusion(f32[4,3,512,512]{2,3,1,0:T(8,128)} %copy-done, f32[4,3,512]{2,1,0:T(4,128)S(1)} %log_add_fusion, pred[512]{0:T(512)(128)(4,1)S(1)} %iota_compare_fusion), kind=kLoop, calls=%fused_computation.13 | loop fusion | flops 12582912 | bytes 18899456 | tf_op jit(solution)/shard_map/convert_element_type | solution.py:183
  124.1 4.0 %convolution_convert_fusion.5 = bf16[4,3,64,512]{3,2,1,0:T(8,128)(2,1)S(1)} fusion(bf16[4,512,3,64]{1,3,2,0:T(8,128)(2,1)S(1)} %bitcast.357, bf16[4,3,512,512]{2,3,1,0:T(8,128)(2,1)} %fusion.2), kind=kOutput, calls=%fused_computation.118 | convolution fusion | flops 403046400 | bytes 7864320 | tf_op jit(solution)/shard_map/kphqs,kpshd->kpqhd/dot_general | solution.py:20
  131.3 18.6 %fusion.12 = (bf16[4,512,768]{2,1,0:T(8,128)(2,1)S(1)}, f32[4,512,768]{2,1,0:T(8,128)}, f32[4,768,512]{1,2,0:T(8,128)}) fusion(f32[4,768]{1,0:T(4,128)S(1)} %fusion.71, bf16[3,768,768]{2,1,0:T(8,128)(2,1)S(1)} %bitcast.364, bf16[1,768,768]{2,1,0:T(8,128)(2,1)S(1)} %bitcast.436, f32[512,768]{1,0:T(8,128)S(1)} %get-tuple-element.76, ...), kind=kOutput, calls=%fused_computation.30 | convolution fusion | flops 2531131392 | bytes 22042624 | tf_op jit(solution)/shard_map/md,kdf->kmf/dot_general | solution.py:20
  149.9 2.8 fusion.98
  155.4 9.6 %convert_reduce_fusion = (f32[4,768]{1,0:T(4,128)S(1)}, bf16[4,512,768]{2,1,0:T(8,128)(2,1)}) fusion(f32[4,512,768]{2,1,0:T(8,128)} %get-tuple-element.39, f32[512,768]{1,0:T(8,128)S(1)} %get-tuple-element.35, bf16[3,768,768]{2,1,0:T(8,128)(2,1)S(1)} %bitcast.367, bf16[1,768,768]{2,1,0:T(8,128)(2,1)S(1)} %bitcast.434, ...), kind=kOutput, calls=%fused_computation.31 | convolution fusion | flops 2445407232 | bytes 22044672 | tf_op jit(solution)/shard_map/md,kfd->kmf/dot_general | solution.py:20
  165.0 5.4 %multiply_reduce_fusion.1 = (f32[768]{0:T(1024)S(1)}, f32[512]{0:T(512)S(1)}, f32[512]{0:T(512)S(1)}, f32[768]{0:T(1024)S(1)}, f32[512,768]{1,0:T(8,128)S(1)}) fusion(f32[512,768]{1,0:T(8,128)S(1)} %get-tuple-element.76, f32[512]{0:T(512)S(1)} %add_rsqrt_fusion.1, f32[512]{0:T(512)S(1)} %broadcast_multiply_fusion.5, f32[768]{0:T(1024)S(1)} %convert_element_type.317, ...), kind=kOutput, calls=%fused_computation.104 | convolution fusion | flops 2422208000 | bytes 12600320 | tf_op jit(solution)/shard_map/kmf,kdf->md/dot_general | solution.py:20
  172.8 2.9 convert_reduce_fusion.2
  175.7 5.6 %multiply_reduce_fusion = (f32[4,3,512]{2,1,0:T(4,128)S(1)}, f32[4,3,512,512]{2,3,1,0:T(8,128)S(1)}) fusion(f32[4,3,512,512]{2,3,1,0:T(8,128)S(1)} %bitcast.342, f32[4,3,512]{2,1,0:T(4,128)S(1)} %log_add_fusion, pred[512]{0:T(512)(128)(4,1)S(1)} %iota_compare_fusion, bf16[4,512,3,64]{1,3,2,0:T(8,128)(2,1)} %bitcast.361, bf16[4,512,3,64]{1,3,2,0:T(8,128)(2,1)} %bitcast.358), kind=kOutput, calls=%fused_computation.4 | convolution fusion | flops 418375680 | bytes 26788352 | tf_op jit(solution)/shard_map/kpqhd,kpshd->kphqs/dot_general | solution.py:20
  181.3 5.8 %multiply_convert_fusion = bf16[4,3,512,512]{2,3,1,0:T(8,128)(2,1)} fusion(f32[4,3,512,512]{2,3,1,0:T(8,128)S(1)} %get-tuple-element.82, f32[4,3,512,512]{2,3,1,0:T(8,128)S(1)} %bitcast.342, f32[4,3,512]{2,1,0:T(4,128)S(1)} %get-tuple-element.81, f32[4,3,512]{2,1,0:T(4,128)S(1)} %log_add_fusion, pred[512]{0:T(512)(128)(4,1)S(1)} %iota_compare_fusion), kind=kLoop, calls=%fused_computation.3 | loop fusion | flops 18874368 | bytes 31506944 | tf_op jit(solution)/shard_map/convert_element_type | solution.py:225
  187.1 4.9 %multiply_convert_fusion.1 = bf16[4,3,64,512]{3,2,1,0:T(8,128)(2,1)S(1)} fusion(bf16[4,512,3,64]{1,3,2,0:T(8,128)(2,1)S(1)} %bitcast.356, bf16[4,3,512,512]{2,3,1,0:T(8,128)(2,1)} %multiply_convert_fusion), kind=kOutput, calls=%fused_computation.105 | convolution fusion | flops 403439616 | bytes 7864320 | tf_op jit(solution)/shard_map/kphqs,kpqhd->kpshd/dot_general | solution.py:20
  195.5 3.1 convert_bitcast_fusion
  198.7 3.0 convolution_convert_fusion
  201.8 3.8 convolution_convert_fusion.1
  205.6 2.3 pad_maximum_fusion.3
  207.9 1.7 dynamic-slice_bitcast_fusion.1
  210.8 3.9 %pad_maximum_fusion = bf16[4,768,1536]{1,2,0:T(8,128)(2,1)} fusion(bf16[4,768,768]{1,2,0:T(8,128)(2,1)S(1)} %convert_bitcast_fusion, bf16[4,768,768]{1,2,0:T(8,128)(2,1)S(1)} %convolution_convert_fusion), kind=kLoop, calls=%fused_computation.10 | loop fusion | flops 18874368 | bytes 18874368 | tf_op jit(solution)/shard_map/concatenate | solution.py:211
  214.7 12.8 %copy.76 = bf16[4,768,1536]{2,1,0:T(8,128)(2,1)} copy(bf16[4,768,1536]{1,2,0:T(8,128)(2,1)} %pad_maximum_fusion) | data formatting | bytes 18874368 | tf_op jit(solution)/shard_map/concatenate | solution.py:211
  227.6 4.9 %dynamic-slice_bitcast_fusion = bf16[4,2,2,96,1536]{4,3,2,1,0:T(8,128)(2,1)} fusion(bf16[4,2,2,2,96,1536]{5,4,3,2,1,0:T(8,128)(2,1)} %bitcast.345, s32[]{:T(128)S(6)} %select_n.497), kind=kLoop, calls=%fused_computation.52 | loop fusion | bytes 9437188 | tf_op jit(solution)/shard_map/jit(dynamic_index_in_dim)/squeeze | solution.py:79
  235.7 4.9 %collective-permute-done.33 = f32[12,768]{1,0:T(8,128)S(1)} collective-permute-done((f32[12,768]{1,0:T(8,128)S(1)}, f32[12,768]{1,0:T(8,128)S(1)}, u32[]{:S(2)}, u32[]{:S(2)}) %collective-permute-start.33) | collective-permute-done | bytes 36896 | tf_op jit(solution)/shard_map/ppermute | solution.py:41
  241.8 1.7 collective-permute-done.34
  243.9 2.7 collective-permute-done.35
  246.6 5.3 %collective-permute-start.36 = (f32[12,768]{1,0:T(8,128)S(1)}, f32[12,768]{1,0:T(8,128)S(1)}, u32[]{:S(2)}, u32[]{:S(2)}) collective-permute-start(f32[12,768]{1,0:T(8,128)S(1)} %add.305), channel_id=1, source_target_pairs={{0,1},{1,0},{2,3},{3,2},{4,5},{5,4},{6,7},{7,6},{8,9},{9,8},{10,11... | collective-permute-start | bytes 110600 | tf_op jit(solution)/shard_map/ppermute | solution.py:126
  253.5 3.1 fusion.25
  259.2 2.9 fusion.43
  262.1 5.5 %collective-permute-done.25 = bf16[2,2,96,768]{3,2,1,0:T(8,128)(2,1)S(1)} collective-permute-done((bf16[2,2,96,768]{3,2,1,0:T(8,128)(2,1)S(1)}, bf16[2,2,96,768]{3,2,1,0:T(8,128)(2,1)S(1)}, u32[]{:S(2)}, u32[]{:S(2)}) %collective-permute-start.25) | collective-permute-done | bytes 589856 | tf_op jit(solution)/shard_map/ppermute | solution.py:41
  269.7 5.9 %collective-permute-done.26 = bf16[2,96,768]{2,1,0:T(8,128)(2,1)S(1)} collective-permute-done((bf16[2,96,768]{2,1,0:T(8,128)(2,1)S(1)}, bf16[2,96,768]{2,1,0:T(8,128)(2,1)S(1)}, u32[]{:S(2)}, u32[]{:S(2)}) %collective-permute-start.26) | collective-permute-done | bytes 294944 | tf_op jit(solution)/shard_map/ppermute | solution.py:41
  276.4 2.6 collective-permute-start.28
  280.0 3.8 fusion.1
  285.3 1.9 collective-permute-start.42
  298.0 11.0 %collective-permute-done.42 = bf16[2,2,96,1536]{3,2,1,0:T(8,128)(2,1)} collective-permute-done((bf16[2,2,96,1536]{3,2,1,0:T(8,128)(2,1)}, bf16[2,2,96,1536]{3,2,1,0:T(8,128)(2,1)}, u32[]{:S(2)}, u32[]{:S(2)}) %collective-permute-start.42) | collective-permute-done | bytes 1179680 | tf_op jit(solution)/shard_map/ppermute | solution.py:41
  310.6 2.1 collective-permute-start.43
  312.8 1.5 fusion.32
  314.6 16.8 %collective-permute-done.43 = bf16[2,96,1536]{2,1,0:T(8,128)(2,1)S(1)} collective-permute-done((bf16[2,96,1536]{2,1,0:T(8,128)(2,1)S(1)}, bf16[2,96,1536]{2,1,0:T(8,128)(2,1)S(1)}, u32[]{:S(2)}, u32[]{:S(2)}) %collective-permute-start.43) | collective-permute-done | bytes 589856 | tf_op jit(solution)/shard_map/ppermute | solution.py:41
  331.6 1.8 collective-permute-start.45
  333.4 2.7 collective-permute-start.44
  338.1 17.4 %collective-permute-done.44 = bf16[96,1536]{1,0:T(8,128)(2,1)S(1)} collective-permute-done((bf16[96,1536]{1,0:T(8,128)(2,1)S(1)}, bf16[96,1536]{1,0:T(8,128)(2,1)S(1)}, u32[]{:S(2)}, u32[]{:S(2)}) %collective-permute-start.44) | collective-permute-done | bytes 294944 | tf_op jit(solution)/shard_map/ppermute | solution.py:45
  355.5 5.4 %collective-permute-done.41 = bf16[96,1536]{1,0:T(8,128)(2,1)S(1)} collective-permute-done((bf16[96,1536]{1,0:T(8,128)(2,1)S(1)}, bf16[96,1536]{1,0:T(8,128)(2,1)S(1)}, u32[]{:S(2)}, u32[]{:S(2)}) %collective-permute-start.41) | collective-permute-done | bytes 294944 | tf_op jit(solution)/shard_map/ppermute | solution.py:45
  362.2 1.7 collective-permute-start.32
  363.9 1.9 collective-permute-start.46
  366.0 3.2 collective-permute-done.48
  369.2 8.1 %collective-permute-done.47 = bf16[96,1536]{1,0:T(8,128)(2,1)S(1)} collective-permute-done((bf16[96,1536]{1,0:T(8,128)(2,1)S(1)}, bf16[96,1536]{1,0:T(8,128)(2,1)S(1)}, u32[]{:S(2)}, u32[]{:S(2)}) %collective-permute-start.47) | collective-permute-done | bytes 294944 | tf_op jit(solution)/shard_map/ppermute | solution.py:41
  381.4 2.5 fusion.93
  (320 shorter events, 70.8 us)
Async XLA Ops:
  1.6 15.2 %copy-start.33 = (bf16[768]{0:T(1024)(128)(2,1)S(1)}, bf16[768]{0:T(1024)(128)(2,1)}, u32[]{:S(2)}) copy-start(bf16[768]{0:T(1024)(128)(2,1)} %param.30) | copy-start | bytes 4612
  1.6 15.2 %copy-start.34 = (bf16[768]{0:T(1024)(128)(2,1)S(1)}, bf16[768]{0:T(1024)(128)(2,1)}, u32[]{:S(2)}) copy-start(bf16[768]{0:T(1024)(128)(2,1)} %param.29) | copy-start | bytes 4612
  1.7 15.2 %copy-start.35 = (bf16[768]{0:T(1024)(128)(2,1)S(1)}, bf16[768]{0:T(1024)(128)(2,1)}, u32[]{:S(2)}) copy-start(bf16[768]{0:T(1024)(128)(2,1)} %param.35) | copy-start | bytes 4612
  1.7 15.2 %copy-start.36 = (bf16[768]{0:T(1024)(128)(2,1)S(1)}, bf16[768]{0:T(1024)(128)(2,1)}, u32[]{:S(2)}) copy-start(bf16[768]{0:T(1024)(128)(2,1)} %param.36) | copy-start | bytes 4612
  1.7 12.3 %collective-permute-start.9 = (bf16[96,768]{1,0:T(8,128)(2,1)S(1)}, bf16[96,768]{1,0:T(8,128)(2,1)S(1)}, u32[]{:S(2)}, u32[]{:S(2)}) collective-permute-start(bf16[96,768]{1,0:T(8,128)(2,1)S(1)} %constant_dynamic-slice_fusion.8), channel_id=1, source_target_pairs={{0,3},{1,0},{2,1},{3,2},{4,7},{5,4},{6,5},{7,6},{8,11},{9,8},{10,9... | collective-permute-start | bytes 442376 | tf_op jit(solution)/shard_map/ppermute | solution.py:45
  1.9 15.0 %collective-permute-start.8 = (bf16[96,768]{1,0:T(8,128)(2,1)S(1)}, bf16[96,768]{1,0:T(8,128)(2,1)S(1)}, u32[]{:S(2)}, u32[]{:S(2)}) collective-permute-start(bf16[96,768]{1,0:T(8,128)(2,1)S(1)} %constant_dynamic-slice_fusion.8), channel_id=1, source_target_pairs={{0,2},{1,3},{2,0},{3,1},{4,6},{5,7},{6,4},{7,5},{8,10},{9,11},{10,... | collective-permute-start | bytes 442376 | tf_op jit(solution)/shard_map/ppermute | solution.py:45
  4.2 18.5 %collective-permute-start.7 = (bf16[96,768]{1,0:T(8,128)(2,1)S(1)}, bf16[96,768]{1,0:T(8,128)(2,1)S(1)}, u32[]{:S(2)}, u32[]{:S(2)}) collective-permute-start(bf16[96,768]{1,0:T(8,128)(2,1)S(1)} %constant_dynamic-slice_fusion.8), channel_id=1, source_target_pairs={{0,1},{1,2},{2,3},{3,0},{4,5},{5,6},{6,7},{7,4},{8,9},{9,10},{10,1... | collective-permute-start | bytes 442376 | tf_op jit(solution)/shard_map/ppermute | solution.py:45
  7.3 18.6 %collective-permute-start.16 = (bf16[96,768]{1,0:T(8,128)(2,1)S(1)}, bf16[96,768]{1,0:T(8,128)(2,1)S(1)}, u32[]{:S(2)}, u32[]{:S(2)}) collective-permute-start(bf16[96,768]{1,0:T(8,128)(2,1)S(1)} %constant_dynamic-slice_fusion.7), channel_id=1, source_target_pairs={{0,3},{1,0},{2,1},{3,2},{4,7},{5,4},{6,5},{7,6},{8,11},{9,8},{10,9... | collective-permute-start | bytes 442376 | tf_op jit(solution)/shard_map/ppermute | solution.py:45
  7.4 24.9 %collective-permute-start.15 = (bf16[96,768]{1,0:T(8,128)(2,1)S(1)}, bf16[96,768]{1,0:T(8,128)(2,1)S(1)}, u32[]{:S(2)}, u32[]{:S(2)}) collective-permute-start(bf16[96,768]{1,0:T(8,128)(2,1)S(1)} %constant_dynamic-slice_fusion.7), channel_id=1, source_target_pairs={{0,2},{1,3},{2,0},{3,1},{4,6},{5,7},{6,4},{7,5},{8,10},{9,11},{10,... | collective-permute-start | bytes 442376 | tf_op jit(solution)/shard_map/ppermute | solution.py:45
  12.1 89.9 %copy-start.15 = (bf16[1,768,768]{2,1,0:T(8,128)(2,1)}, bf16[1,768,768]{2,1,0:T(8,128)(2,1)S(1)}, u32[]{:S(2)}) copy-start(bf16[1,768,768]{2,1,0:T(8,128)(2,1)S(1)} %get-tuple-element.58) | copy-start | bytes 3538948
  14.0 22.5 %collective-permute-start.14 = (bf16[96,768]{1,0:T(8,128)(2,1)S(1)}, bf16[96,768]{1,0:T(8,128)(2,1)S(1)}, u32[]{:S(2)}, u32[]{:S(2)}) collective-permute-start(bf16[96,768]{1,0:T(8,128)(2,1)S(1)} %constant_dynamic-slice_fusion.7), channel_id=1, source_target_pairs={{0,1},{1,2},{2,3},{3,0},{4,5},{5,6},{6,7},{7,4},{8,9},{9,10},{10,1... | collective-permute-start | bytes 442376 | tf_op jit(solution)/shard_map/ppermute | solution.py:45
  16.9 23.2 %collective-permute-start.2 = (bf16[112,768]{1,0:T(8,128)(2,1)S(1)}, bf16[112,768]{1,0:T(8,128)(2,1)S(1)}, u32[]{:S(2)}, u32[]{:S(2)}) collective-permute-start(bf16[112,768]{1,0:T(8,128)(2,1)S(1)} %pad_maximum_fusion.20), channel_id=1, source_target_pairs={{0,3},{1,0},{2,1},{3,2},{4,7},{5,4},{6,5},{7,6},{8,11},{9,8},{10,9... | collective-permute-start | bytes 516104 | tf_op jit(solution)/shard_map/ppermute | solution.py:45
  22.7 18.6 %collective-permute-start.1 = (bf16[112,768]{1,0:T(8,128)(2,1)S(1)}, bf16[112,768]{1,0:T(8,128)(2,1)S(1)}, u32[]{:S(2)}, u32[]{:S(2)}) collective-permute-start(bf16[112,768]{1,0:T(8,128)(2,1)S(1)} %pad_maximum_fusion.20), channel_id=1, source_target_pairs={{0,2},{1,3},{2,0},{3,1},{4,6},{5,7},{6,4},{7,5},{8,10},{9,11},{10,... | collective-permute-start | bytes 516104 | tf_op jit(solution)/shard_map/ppermute | solution.py:45
  25.9 18.0 %collective-permute-start = (bf16[112,768]{1,0:T(8,128)(2,1)S(1)}, bf16[112,768]{1,0:T(8,128)(2,1)S(1)}, u32[]{:S(2)}, u32[]{:S(2)}) collective-permute-start(bf16[112,768]{1,0:T(8,128)(2,1)S(1)} %pad_maximum_fusion.20), channel_id=1, source_target_pairs={{0,1},{1,2},{2,3},{3,0},{4,5},{5,6},{6,7},{7,4},{8,9},{9,10},{10,1... | collective-permute-start | bytes 516104 | tf_op jit(solution)/shard_map/ppermute | solution.py:45
  32.3 12.1 %collective-permute-start.12 = (bf16[3,96,768]{2,1,0:T(8,128)(2,1)S(1)}, bf16[3,96,768]{2,1,0:T(8,128)(2,1)S(1)}, u32[]{:S(2)}, u32[]{:S(2)}) collective-permute-start(bf16[3,96,768]{2,1,0:T(8,128)(2,1)S(1)} %get-tuple-element.66), channel_id=1, source_target_pairs={{0,24},{4,28},{8,16},{12,20},{16,8},{20,12},{24,0},{28,4},{1,25},{... | collective-permute-start | bytes 1327112 | tf_op jit(solution)/shard_map/ppermute | solution.py:41
  36.5 20.7 %collective-permute-start.11 = (bf16[3,96,768]{2,1,0:T(8,128)(2,1)S(1)}, bf16[3,96,768]{2,1,0:T(8,128)(2,1)S(1)}, u32[]{:S(2)}, u32[]{:S(2)}) collective-permute-start(bf16[3,96,768]{2,1,0:T(8,128)(2,1)S(1)} %get-tuple-element.66), channel_id=1, source_target_pairs={{0,16},{4,20},{8,24},{12,28},{16,0},{20,4},{24,8},{28,12},{1,17},{... | collective-permute-start | bytes 1327112 | tf_op jit(solution)/shard_map/ppermute | solution.py:41
  40.1 17.5 %collective-permute-start.10 = (bf16[3,96,768]{2,1,0:T(8,128)(2,1)S(1)}, bf16[3,96,768]{2,1,0:T(8,128)(2,1)S(1)}, u32[]{:S(2)}, u32[]{:S(2)}) collective-permute-start(bf16[3,96,768]{2,1,0:T(8,128)(2,1)S(1)} %get-tuple-element.66), channel_id=1, source_target_pairs={{0,8},{4,12},{8,0},{12,4},{16,24},{20,28},{24,16},{28,20},{1,9},{5... | collective-permute-start | bytes 1327112 | tf_op jit(solution)/shard_map/ppermute | solution.py:41
  41.3 20.5 %collective-permute-start.19 = (bf16[3,96,768]{2,1,0:T(8,128)(2,1)S(1)}, bf16[3,96,768]{2,1,0:T(8,128)(2,1)S(1)}, u32[]{:S(2)}, u32[]{:S(2)}) collective-permute-start(bf16[3,96,768]{2,1,0:T(8,128)(2,1)S(1)} %get-tuple-element.64), channel_id=1, source_target_pairs={{0,24},{4,28},{8,16},{12,20},{16,8},{20,12},{24,0},{28,4},{1,25},{... | collective-permute-start | bytes 1327112 | tf_op jit(solution)/shard_map/ppermute | solution.py:41
  43.9 32.3 %collective-permute-start.18 = (bf16[3,96,768]{2,1,0:T(8,128)(2,1)S(1)}, bf16[3,96,768]{2,1,0:T(8,128)(2,1)S(1)}, u32[]{:S(2)}, u32[]{:S(2)}) collective-permute-start(bf16[3,96,768]{2,1,0:T(8,128)(2,1)S(1)} %get-tuple-element.64), channel_id=1, source_target_pairs={{0,16},{4,20},{8,24},{12,28},{16,0},{20,4},{24,8},{28,12},{1,17},{... | collective-permute-start | bytes 1327112 | tf_op jit(solution)/shard_map/ppermute | solution.py:41
  44.4 32.7 %collective-permute-start.17 = (bf16[3,96,768]{2,1,0:T(8,128)(2,1)S(1)}, bf16[3,96,768]{2,1,0:T(8,128)(2,1)S(1)}, u32[]{:S(2)}, u32[]{:S(2)}) collective-permute-start(bf16[3,96,768]{2,1,0:T(8,128)(2,1)S(1)} %get-tuple-element.64), channel_id=1, source_target_pairs={{0,8},{4,12},{8,0},{12,4},{16,24},{20,28},{24,16},{28,20},{1,9},{5... | collective-permute-start | bytes 1327112 | tf_op jit(solution)/shard_map/ppermute | solution.py:41
  57.3 23.6 %collective-permute-start.5 = (bf16[3,96,768]{2,1,0:T(8,128)(2,1)S(1)}, bf16[3,96,768]{2,1,0:T(8,128)(2,1)S(1)}, u32[]{:S(2)}, u32[]{:S(2)}) collective-permute-start(bf16[3,96,768]{2,1,0:T(8,128)(2,1)S(1)} %get-tuple-element.62), channel_id=1, source_target_pairs={{0,24},{4,28},{8,16},{12,20},{16,8},{20,12},{24,0},{28,4},{1,25},{... | collective-permute-start | bytes 1327112 | tf_op jit(solution)/shard_map/ppermute | solution.py:41
  57.6 35.1 %collective-permute-start.4 = (bf16[3,96,768]{2,1,0:T(8,128)(2,1)S(1)}, bf16[3,96,768]{2,1,0:T(8,128)(2,1)S(1)}, u32[]{:S(2)}, u32[]{:S(2)}) collective-permute-start(bf16[3,96,768]{2,1,0:T(8,128)(2,1)S(1)} %get-tuple-element.62), channel_id=1, source_target_pairs={{0,16},{4,20},{8,24},{12,28},{16,0},{20,4},{24,8},{28,12},{1,17},{... | collective-permute-start | bytes 1327112 | tf_op jit(solution)/shard_map/ppermute | solution.py:41
  61.8 31.0 %collective-permute-start.3 = (bf16[3,96,768]{2,1,0:T(8,128)(2,1)S(1)}, bf16[3,96,768]{2,1,0:T(8,128)(2,1)S(1)}, u32[]{:S(2)}, u32[]{:S(2)}) collective-permute-start(bf16[3,96,768]{2,1,0:T(8,128)(2,1)S(1)} %get-tuple-element.62), channel_id=1, source_target_pairs={{0,8},{4,12},{8,0},{12,4},{16,24},{20,28},{24,16},{28,20},{1,9},{5... | collective-permute-start | bytes 1327112 | tf_op jit(solution)/shard_map/ppermute | solution.py:41
  76.2 19.2 %collective-permute-start.13 = (bf16[3,2,2,96,768]{4,3,0,2,1:T(8,128)(2,1)S(1)}, bf16[3,2,2,96,768]{4,3,0,2,1:T(8,128)(2,1)S(1)}, u32[]{:S(2)}, u32[]{:S(2)}) collective-permute-start(bf16[3,2,2,96,768]{4,3,0,2,1:T(8,128)(2,1)S(1)} %maximum_select_fusion.6), channel_id=1, source_target_pairs={{0,4},{4,0},{8,12},{12,8},{16,20},{20,16},{24,28},{28,24},{1,5},{5... | collective-permute-start | bytes 5308424 | tf_op jit(solution)/shard_map/ppermute | solution.py:41
  77.6 20.5 %collective-permute-start.20 = (bf16[3,2,2,96,768]{4,3,0,2,1:T(8,128)(2,1)S(1)}, bf16[3,2,2,96,768]{4,3,0,2,1:T(8,128)(2,1)S(1)}, u32[]{:S(2)}, u32[]{:S(2)}) collective-permute-start(bf16[3,2,2,96,768]{4,3,0,2,1:T(8,128)(2,1)S(1)} %maximum_select_fusion.8), channel_id=1, source_target_pairs={{0,4},{4,0},{8,12},{12,8},{16,20},{20,16},{24,28},{28,24},{1,5},{5... | collective-permute-start | bytes 5308424 | tf_op jit(solution)/shard_map/ppermute | solution.py:41
  93.3 7.4 %collective-permute-start.6 = (bf16[3,2,2,96,768]{4,3,0,2,1:T(8,128)(2,1)S(1)}, bf16[3,2,2,96,768]{4,3,0,2,1:T(8,128)(2,1)S(1)}, u32[]{:S(2)}, u32[]{:S(2)}) collective-permute-start(bf16[3,2,2,96,768]{4,3,0,2,1:T(8,128)(2,1)S(1)} %maximum_select_fusion.5), channel_id=1, source_target_pairs={{0,4},{4,0},{8,12},{12,8},{16,20},{20,16},{24,28},{28,24},{1,5},{5... | collective-permute-start | bytes 5308424 | tf_op jit(solution)/shard_map/ppermute | solution.py:41
  106.1 18.0 %copy-start.7 = (bf16[4,512,192]{1,2,0:T(8,128)(2,1)}, bf16[4,512,192]{1,2,0:T(8,128)(2,1)S(1)}, u32[]{:S(2)}) copy-start(bf16[4,512,192]{1,2,0:T(8,128)(2,1)S(1)} %get-tuple-element.45) | copy-start | bytes 2359300
  129.6 40.9 %copy-start.13 = (f32[512,768]{1,0:T(8,128)}, f32[512,768]{1,0:T(8,128)S(1)}, u32[]{:S(2)}) copy-start(f32[512,768]{1,0:T(8,128)S(1)} %get-tuple-element.76) | copy-start | bytes 4718596
  131.3 18.7 %copy-start.18 = (bf16[3,2,2,2,96,768]{5,4,3,2,1,0:T(8,128)(2,1)S(1)}, bf16[3,2,2,2,96,768]{5,4,3,2,1,0:T(8,128)(2,1)}, u32[]{:S(2)}) copy-start(bf16[3,2,2,2,96,768]{5,4,3,2,1,0:T(8,128)(2,1)} %copy.68) | copy-start | bytes 10616836
  131.3 18.7 %copy-start.29 = (bf16[768,768]{1,0:T(8,128)(2,1)S(1)}, bf16[768,768]{1,0:T(8,128)(2,1)}, u32[]{:S(2)}) copy-start(bf16[768,768]{1,0:T(8,128)(2,1)} %param.33) | copy-start | bytes 3538948
  153.8 18.9 %slice-start.3 = ((s8[6291456]{0:T(1024)(128)(4,1)}), s8[4194304]{0:T(1024)(128)(4,1)S(1)}, s32[]{:S(2)}) async-start(s8[6291456]{0:T(1024)(128)(4,1)} %bitcast.343), calls=%async_computation.3 | async-start | bytes 8388608
  155.4 17.4 %slice-start.4 = ((s8[6291456]{0:T(1024)(128)(4,1)}), s8[2097152]{0:T(1024)(128)(4,1)S(1)}, s32[]{:S(2)}) async-start(s8[6291456]{0:T(1024)(128)(4,1)} %bitcast.343), calls=%async_computation.4 | async-start | bytes 4194304
  210.8 42.7 %collective-permute-start.21 = (bf16[4,2,2,96,768]{4,3,2,1,0:T(8,128)(2,1)}, bf16[4,2,2,96,768]{4,3,2,1,0:T(8,128)(2,1)}, u32[]{:S(2)}, u32[]{:S(2)}) collective-permute-start(bf16[4,2,2,96,768]{4,3,2,1,0:T(8,128)(2,1)} %dynamic-slice_bitcast_fusion.1), channel_id=1, source_target_pairs={{0,4},{4,0},{8,12},{12,8},{16,20},{20,16},{24,28},{28,24},{1,5},{5... | collective-permute-start | bytes 7077896 | tf_op jit(solution)/shard_map/ppermute | solution.py:41
  232.5 47.4 %collective-permute-start.38 = (bf16[4,2,2,96,1536]{4,3,2,1,0:T(8,128)(2,1)}, bf16[4,2,2,96,1536]{4,3,2,1,0:T(8,128)(2,1)}, u32[]{:S(2)}, u32[]{:S(2)}) collective-permute-start(bf16[4,2,2,96,1536]{4,3,2,1,0:T(8,128)(2,1)} %dynamic-slice_bitcast_fusion), channel_id=1, source_target_pairs={{0,4},{4,0},{8,12},{12,8},{16,20},{20,16},{24,28},{28,24},{1,5},{5... | collective-permute-start | bytes 14155784 | tf_op jit(solution)/shard_map/ppermute | solution.py:41
  235.6 5.0 %collective-permute-start.33 = (f32[12,768]{1,0:T(8,128)S(1)}, f32[12,768]{1,0:T(8,128)S(1)}, u32[]{:S(2)}, u32[]{:S(2)}) collective-permute-start(f32[12,768]{1,0:T(8,128)S(1)} %reshape.1831), channel_id=1, source_target_pairs={{0,4},{4,0},{8,12},{12,8},{16,20},{20,16},{24,28},{28,24},{1,5},{5... | collective-permute-start | bytes 110600 | tf_op jit(solution)/shard_map/ppermute | solution.py:41
  240.6 2.9 collective-permute-start.34
  243.6 3.0 collective-permute-start.35
  246.6 6.8 %collective-permute-start.36 = (f32[12,768]{1,0:T(8,128)S(1)}, f32[12,768]{1,0:T(8,128)S(1)}, u32[]{:S(2)}, u32[]{:S(2)}) collective-permute-start(f32[12,768]{1,0:T(8,128)S(1)} %add.305), channel_id=1, source_target_pairs={{0,1},{1,0},{2,3},{3,2},{4,5},{5,4},{6,7},{7,6},{8,9},{9,8},{10,11... | collective-permute-start | bytes 110600 | tf_op jit(solution)/shard_map/ppermute | solution.py:126
  253.4 8.7 %collective-permute-start.37 = (f32[12,768]{1,0:T(8,128)S(1)}, f32[12,768]{1,0:T(8,128)S(1)}, u32[]{:S(2)}, u32[]{:S(2)}) collective-permute-start(f32[12,768]{1,0:T(8,128)S(1)} %add.306), channel_id=1, source_target_pairs={{0,2},{1,3},{2,0},{3,1},{4,6},{5,7},{6,4},{7,5},{8,10},{9,11},{10,... | collective-permute-start | bytes 110600 | tf_op jit(solution)/shard_map/ppermute | solution.py:126
  256.8 10.9 %collective-permute-start.25 = (bf16[2,2,96,768]{3,2,1,0:T(8,128)(2,1)S(1)}, bf16[2,2,96,768]{3,2,1,0:T(8,128)(2,1)S(1)}, u32[]{:S(2)}, u32[]{:S(2)}) collective-permute-start(bf16[2,2,96,768]{3,2,1,0:T(8,128)(2,1)S(1)} %dynamic-slice_bitcast_fusion.5), channel_id=1, source_target_pairs={{0,16},{4,20},{8,24},{12,28},{16,0},{20,4},{24,8},{28,12},{1,17},{... | collective-permute-start | bytes 1769480 | tf_op jit(solution)/shard_map/ppermute | solution.py:41
  257.3 22.7 %slice-start.5 = ((s8[9437184]{0:T(1024)(128)(4,1)}), s8[4194304]{0:T(1024)(128)(4,1)S(1)}, s32[]{:S(2)}) async-start(s8[9437184]{0:T(1024)(128)(4,1)} %bitcast.346), calls=%async_computation.5 | async-start | bytes 8388608
  257.3 22.7 %slice-start.6 = ((s8[9437184]{0:T(1024)(128)(4,1)}), s8[4194304]{0:T(1024)(128)(4,1)S(1)}, s32[]{:S(2)}) async-start(s8[9437184]{0:T(1024)(128)(4,1)} %bitcast.346), calls=%async_computation.6 | async-start | bytes 8388608
  257.3 22.7 %slice-start.7 = ((s8[9437184]{0:T(1024)(128)(4,1)}), s8[1048576]{0:T(1024)(128)(4,1)S(1)}, s32[]{:S(2)}) async-start(s8[9437184]{0:T(1024)(128)(4,1)} %bitcast.346), calls=%async_computation.7 | async-start | bytes 2097152
  257.3 11.2 %collective-permute-start.22 = (bf16[2,2,96,768]{3,2,0,1:T(8,128)(2,1)S(1)}, bf16[2,2,96,768]{3,2,0,1:T(8,128)(2,1)S(1)}, u32[]{:S(2)}, u32[]{:S(2)}) collective-permute-start(bf16[2,2,96,768]{3,2,0,1:T(8,128)(2,1)S(1)} %bitcast.416), channel_id=1, source_target_pairs={{0,8},{4,12},{8,0},{12,4},{16,24},{20,28},{24,16},{28,20},{1,9},{5... | collective-permute-start | bytes 1769480 | tf_op jit(solution)/shard_map/ppermute | solution.py:41
  267.9 7.7 %collective-permute-start.26 = (bf16[2,96,768]{2,1,0:T(8,128)(2,1)S(1)}, bf16[2,96,768]{2,1,0:T(8,128)(2,1)S(1)}, u32[]{:S(2)}, u32[]{:S(2)}) collective-permute-start(bf16[2,96,768]{2,1,0:T(8,128)(2,1)S(1)} %dynamic-slice_bitcast_fusion.6), channel_id=1, source_target_pairs={{0,8},{4,12},{8,0},{12,4},{16,24},{20,28},{24,16},{28,20},{1,9},{5... | collective-permute-start | bytes 884744 | tf_op jit(solution)/shard_map/ppermute | solution.py:41
  268.6 18.6 %collective-permute-start.23 = (bf16[2,96,768]{2,1,0:T(8,128)(2,1)S(1)}, bf16[2,96,768]{2,1,0:T(8,128)(2,1)S(1)}, u32[]{:S(2)}, u32[]{:S(2)}) collective-permute-start(bf16[2,96,768]{2,1,0:T(8,128)(2,1)S(1)} %dynamic-slice_bitcast_fusion.7), channel_id=1, source_target_pairs={{0,16},{4,20},{8,24},{12,28},{16,0},{20,4},{24,8},{28,12},{1,17},{... | collective-permute-start | bytes 884744 | tf_op jit(solution)/shard_map/ppermute | solution.py:41
  276.4 17.6 %collective-permute-start.28 = (bf16[96,768]{1,0:T(8,128)(2,1)}, bf16[96,768]{1,0:T(8,128)(2,1)}, u32[]{:S(2)}, u32[]{:S(2)}) collective-permute-start(bf16[96,768]{1,0:T(8,128)(2,1)} %get-tuple-element.68), channel_id=1, source_target_pairs={{0,1},{1,2},{2,3},{3,0},{4,5},{5,6},{6,7},{7,4},{8,9},{9,10},{10,1... | collective-permute-start | bytes 442376 | tf_op jit(solution)/shard_map/ppermute | solution.py:45
  279.0 15.0 %collective-permute-start.27 = (bf16[96,768]{1,0:T(8,128)(2,1)}, bf16[96,768]{1,0:T(8,128)(2,1)}, u32[]{:S(2)}, u32[]{:S(2)}) collective-permute-start(bf16[96,768]{1,0:T(8,128)(2,1)} %get-tuple-element.67), channel_id=1, source_target_pairs={{0,2},{1,3},{2,0},{3,1},{4,6},{5,7},{6,4},{7,5},{8,10},{9,11},{10,... | collective-permute-start | bytes 442376 | tf_op jit(solution)/shard_map/ppermute | solution.py:45
  285.3 23.7 %collective-permute-start.42 = (bf16[2,2,96,1536]{3,2,1,0:T(8,128)(2,1)}, bf16[2,2,96,1536]{3,2,1,0:T(8,128)(2,1)}, u32[]{:S(2)}, u32[]{:S(2)}) collective-permute-start(bf16[2,2,96,1536]{3,2,1,0:T(8,128)(2,1)} %dynamic-slice_bitcast_fusion.2), channel_id=1, source_target_pairs={{0,16},{4,20},{8,24},{12,28},{16,0},{20,4},{24,8},{28,12},{1,17},{... | collective-permute-start | bytes 3538952 | tf_op jit(solution)/shard_map/ppermute | solution.py:41
  288.0 6.0 %collective-permute-start.24 = (bf16[96,768]{1,0:T(8,128)(2,1)}, bf16[96,768]{1,0:T(8,128)(2,1)}, u32[]{:S(2)}, u32[]{:S(2)}) collective-permute-start(bf16[96,768]{1,0:T(8,128)(2,1)} %slice_bitcast_fusion.9), channel_id=1, source_target_pairs={{0,3},{1,0},{2,1},{3,2},{4,7},{5,4},{6,5},{7,6},{8,11},{9,8},{10,9... | collective-permute-start | bytes 442376 | tf_op jit(solution)/shard_map/ppermute | solution.py:45
  289.4 23.4 %collective-permute-start.39 = (bf16[2,2,96,1536]{3,2,0,1:T(8,128)(2,1)}, bf16[2,2,96,1536]{3,2,0,1:T(8,128)(2,1)}, u32[]{:S(2)}, u32[]{:S(2)}) collective-permute-start(bf16[2,2,96,1536]{3,2,0,1:T(8,128)(2,1)} %bitcast.339), channel_id=1, source_target_pairs={{0,8},{4,12},{8,0},{12,4},{16,24},{20,28},{24,16},{28,20},{1,9},{5... | collective-permute-start | bytes 3538952 | tf_op jit(solution)/shard_map/ppermute | solution.py:41
  295.3 41.0 %collective-permute-start.31 = (bf16[96,768]{1,0:T(8,128)(2,1)S(1)}, bf16[96,768]{1,0:T(8,128)(2,1)S(1)}, u32[]{:S(2)}, u32[]{:S(2)}) collective-permute-start(bf16[96,768]{1,0:T(8,128)(2,1)S(1)} %fusion.70), channel_id=1, source_target_pairs={{0,24},{4,28},{8,16},{12,20},{16,8},{20,12},{24,0},{28,4},{1,25},{... | collective-permute-start | bytes 442376 | tf_op jit(solution)/shard_map/ppermute | solution.py:41
  296.4 40.2 %collective-permute-start.30 = (bf16[96,768]{1,0:T(8,128)(2,1)S(1)}, bf16[96,768]{1,0:T(8,128)(2,1)S(1)}, u32[]{:S(2)}, u32[]{:S(2)}) collective-permute-start(bf16[96,768]{1,0:T(8,128)(2,1)S(1)} %fusion.70), channel_id=1, source_target_pairs={{0,16},{4,20},{8,24},{12,28},{16,0},{20,4},{24,8},{28,12},{1,17},{... | collective-permute-start | bytes 442376 | tf_op jit(solution)/shard_map/ppermute | solution.py:41
  297.8 38.8 %collective-permute-start.29 = (bf16[96,768]{1,0:T(8,128)(2,1)S(1)}, bf16[96,768]{1,0:T(8,128)(2,1)S(1)}, u32[]{:S(2)}, u32[]{:S(2)}) collective-permute-start(bf16[96,768]{1,0:T(8,128)(2,1)S(1)} %fusion.70), channel_id=1, source_target_pairs={{0,8},{4,12},{8,0},{12,4},{16,24},{20,28},{24,16},{28,20},{1,9},{5... | collective-permute-start | bytes 442376 | tf_op jit(solution)/shard_map/ppermute | solution.py:41
  310.6 20.8 %collective-permute-start.43 = (bf16[2,96,1536]{2,1,0:T(8,128)(2,1)S(1)}, bf16[2,96,1536]{2,1,0:T(8,128)(2,1)S(1)}, u32[]{:S(2)}, u32[]{:S(2)}) collective-permute-start(bf16[2,96,1536]{2,1,0:T(8,128)(2,1)S(1)} %dynamic-slice_bitcast_fusion.3), channel_id=1, source_target_pairs={{0,8},{4,12},{8,0},{12,4},{16,24},{20,28},{24,16},{28,20},{1,9},{5... | collective-permute-start | bytes 1769480 | tf_op jit(solution)/shard_map/ppermute | solution.py:41
  314.4 19.0 %collective-permute-start.40 = (bf16[2,96,1536]{2,1,0:T(8,128)(2,1)S(1)}, bf16[2,96,1536]{2,1,0:T(8,128)(2,1)S(1)}, u32[]{:S(2)}, u32[]{:S(2)}) collective-permute-start(bf16[2,96,1536]{2,1,0:T(8,128)(2,1)S(1)} %dynamic-slice_bitcast_fusion.4), channel_id=1, source_target_pairs={{0,16},{4,20},{8,24},{12,28},{16,0},{20,4},{24,8},{28,12},{1,17},{... | collective-permute-start | bytes 1769480 | tf_op jit(solution)/shard_map/ppermute | solution.py:41
  331.6 6.5 %collective-permute-start.45 = (bf16[96,1536]{1,0:T(8,128)(2,1)S(1)}, bf16[96,1536]{1,0:T(8,128)(2,1)S(1)}, u32[]{:S(2)}, u32[]{:S(2)}) collective-permute-start(bf16[96,1536]{1,0:T(8,128)(2,1)S(1)} %get-tuple-element.60), channel_id=1, source_target_pairs={{0,1},{1,2},{2,3},{3,0},{4,5},{5,6},{6,7},{7,4},{8,9},{9,10},{10,1... | collective-permute-start | bytes 884744 | tf_op jit(solution)/shard_map/ppermute | solution.py:45
  333.4 22.1 %collective-permute-start.44 = (bf16[96,1536]{1,0:T(8,128)(2,1)S(1)}, bf16[96,1536]{1,0:T(8,128)(2,1)S(1)}, u32[]{:S(2)}, u32[]{:S(2)}) collective-permute-start(bf16[96,1536]{1,0:T(8,128)(2,1)S(1)} %get-tuple-element.59), channel_id=1, source_target_pairs={{0,2},{1,3},{2,0},{3,1},{4,6},{5,7},{6,4},{7,5},{8,10},{9,11},{10,... | collective-permute-start | bytes 884744 | tf_op jit(solution)/shard_map/ppermute | solution.py:45
  336.3 24.6 %collective-permute-start.41 = (bf16[96,1536]{1,0:T(8,128)(2,1)S(1)}, bf16[96,1536]{1,0:T(8,128)(2,1)S(1)}, u32[]{:S(2)}, u32[]{:S(2)}) collective-permute-start(bf16[96,1536]{1,0:T(8,128)(2,1)S(1)} %slice_bitcast_fusion.5), channel_id=1, source_target_pairs={{0,3},{1,0},{2,1},{3,2},{4,7},{5,4},{6,5},{7,6},{8,11},{9,8},{10,9... | collective-permute-start | bytes 884744 | tf_op jit(solution)/shard_map/ppermute | solution.py:45
  361.0 8.2 %collective-permute-start.48 = (bf16[96,1536]{1,0:T(8,128)(2,1)S(1)}, bf16[96,1536]{1,0:T(8,128)(2,1)S(1)}, u32[]{:S(2)}, u32[]{:S(2)}) collective-permute-start(bf16[96,1536]{1,0:T(8,128)(2,1)S(1)} %fusion.61), channel_id=1, source_target_pairs={{0,24},{4,28},{8,16},{12,20},{16,8},{20,12},{24,0},{28,4},{1,25},{... | collective-permute-start | bytes 884744 | tf_op jit(solution)/shard_map/ppermute | solution.py:41
  362.2 15.1 %collective-permute-start.47 = (bf16[96,1536]{1,0:T(8,128)(2,1)S(1)}, bf16[96,1536]{1,0:T(8,128)(2,1)S(1)}, u32[]{:S(2)}, u32[]{:S(2)}) collective-permute-start(bf16[96,1536]{1,0:T(8,128)(2,1)S(1)} %fusion.61), channel_id=1, source_target_pairs={{0,16},{4,20},{8,24},{12,28},{16,0},{20,4},{24,8},{28,12},{1,17},{... | collective-permute-start | bytes 884744 | tf_op jit(solution)/shard_map/ppermute | solution.py:41
  362.2 16.0 %collective-permute-start.32 = (bf16[2,2,96,768]{3,2,1,0:T(8,128)(2,1)S(1)}, bf16[2,2,96,768]{3,2,1,0:T(8,128)(2,1)S(1)}, u32[]{:S(2)}, u32[]{:S(2)}) collective-permute-start(bf16[2,2,96,768]{3,2,1,0:T(8,128)(2,1)S(1)} %maximum_select_fusion.19), channel_id=1, source_target_pairs={{0,4},{4,0},{8,12},{12,8},{16,20},{20,16},{24,28},{28,24},{1,5},{5... | collective-permute-start | bytes 1769480 | tf_op jit(solution)/shard_map/ppermute | solution.py:41
  363.9 13.4 %collective-permute-start.46 = (bf16[96,1536]{1,0:T(8,128)(2,1)S(1)}, bf16[96,1536]{1,0:T(8,128)(2,1)S(1)}, u32[]{:S(2)}, u32[]{:S(2)}) collective-permute-start(bf16[96,1536]{1,0:T(8,128)(2,1)S(1)} %fusion.61), channel_id=1, source_target_pairs={{0,8},{4,12},{8,0},{12,4},{16,24},{20,28},{24,16},{28,20},{1,9},{5... | collective-permute-start | bytes 884744 | tf_op jit(solution)/shard_map/ppermute | solution.py:41
  377.7 3.0 collective-permute-start.49
  (39 other events, 178.3 us)

commit v2 on v1

v2 whole, which is shorter than its diff:
```python
from functools import partial

import jax
import jax.numpy as jnp
from jax import lax
from jax.experimental import pallas as pl
from jax.experimental.pallas import tpu as pltpu
from jax.sharding import PartitionSpec as P

HD = 64
SEQ = 512
GROUP = 8
LOG2E = 1.4426950408889634
TAIL_P = 0.39
TAIL = (
    0.23532521908406087,
    0.09138841455460205,
    0.6495593986198918,
    -0.6354002786931026,
    0.8866643698688825,
    -0.22753712513305413,
)

epsilon = 1e-12
masked_score = -1000000000.0
low = jnp.bfloat16
wide = jnp.float32
PEAK = 1.1e15


def mm(left, right, left_dim, right_dim):
    return lax.dot_general(
        left, right, (((left_dim,), (right_dim,)), ((), ())), preferred_element_type=wide
    )


def vmem():
    return pl.BlockSpec(memory_space=pltpu.VMEM)


def smem():
    return pl.BlockSpec(memory_space=pltpu.SMEM)


def hbm():
    return pl.BlockSpec(memory_space=pl.ANY)


def cost(microseconds):
    return pl.CostEstimate(
        flops=int(microseconds * 1e-6 * PEAK), bytes_accessed=1 << 20, transcendentals=0
    )


def params(mebibytes):
    return pltpu.CompilerParams(vmem_limit_bytes=mebibytes << 20)


def block(shape, index):
    return pl.BlockSpec(shape, lambda i: index)


def shaped(shape, dtype):
    return jax.ShapeDtypeStruct(shape, dtype)


def masked_pad(length, seq):
    row = lax.broadcasted_iota(jnp.int32, (16, seq), 0)
    key = lax.broadcasted_iota(jnp.int32, (16, seq), 1)
    bias = jnp.where((row == 0) & (key >= length), masked_score, 0.0).astype(low)
    ones = jnp.where(row == 0, 1.0, 0.0).astype(low)
    return bias, ones


def as_column(row, ones):
    first = lax.broadcasted_iota(jnp.int32, (16, row.shape[1]), 0) == 0
    return mm(jnp.where(first, row, 0.0).astype(low), ones, 0, 0)


def group_forward(tokens, weights, bias, length, qkv_ref, ctx_ref, lse_ref):
    local = weights.shape[0] // 4
    seq = tokens.shape[0]
    scale = HD**-0.5 * LOG2E
    key_pad, ones = masked_pad(length, seq)
    joint = mm(weights[: 3 * local], tokens, 1, 1)
    query = (joint[:local] + as_column(bias[:, :local], ones)).astype(low)
    key = joint[local : 2 * local].astype(low)
    value = (joint[2 * local :] + as_column(bias[:, local : 2 * local], ones)).astype(low)
    qkv_ref[:local] = query
    qkv_ref[local : 2 * local] = key
    qkv_ref[2 * local :] = value
    for h in range(local // HD):
        part = slice(h * HD, (h + 1) * HD)
        scores = mm(
            jnp.concatenate([key[part], key_pad], 0), jnp.concatenate([query[part], ones], 0), 0, 0
        )
        top = jnp.max(scores, axis=0, keepdims=True)
        probs = jnp.exp2((scores - top) * scale)
        total = jnp.sum(probs, axis=0, keepdims=True)
        context = mm(value[part], probs.astype(low), 1, 0)
        ctx_ref[part] = (context * (1.0 / total)).astype(low)
        lse_ref[h : h + 1] = top * scale + jnp.log2(total)


def gelu_parts(x):
    t = 1.0 / (1.0 + (TAIL_P * 0.5**0.5) * jnp.abs(x))
    poly = TAIL[-1]
    for factor in TAIL[-2::-1]:
        poly = poly * t + factor
    bell = jnp.exp2(x * x * (-0.5 * LOG2E))
    half = 0.5 * poly * t * bell
    cdf = jnp.where(x >= 0, 1.0 - half, half)
    return x * cdf, cdf + x * bell * (0.5 / jnp.pi) ** 0.5


def norm_parts(values):
    centred = values - jnp.mean(values, axis=1, keepdims=True)
    inverse = lax.rsqrt(jnp.mean(centred * centred, axis=1, keepdims=True) + epsilon)
    return centred * inverse, inverse


def norm_back(scaled, normal, inverse):
    return inverse * (
        scaled
        - jnp.mean(scaled, axis=1, keepdims=True)
        - normal * jnp.mean(scaled * normal, axis=1, keepdims=True)
    )


def piece_copies(info, refs, target, sems):
    copies = []
    for s in range(2):
        first, second, third = refs[3 * s : 3 * s + 3]
        holder = info[1] ^ s
        order = (1 + holder, 2 - holder, 3)
        views = (first, second, third.at[0], third.at[1])
        for view, move in zip(views, (0,) + order):
            rows = view.shape[1]
            start = pl.multiple_of((holder * 4 + (info[2] ^ move)) * rows, rows)
            for entry, k in enumerate(order):
                copies.append(
                    pltpu.make_async_copy(
                        view.at[entry],
                        target.at[k, pl.ds(start, rows), :],
                        sems.at[len(copies)],
                    )
                )
    return copies


def place_pieces(info, value, keep_ref, send_ref, entry):
    rows = value.shape[0] // GROUP
    for p in range(GROUP):
        half, move = p >> 2, (p & 3) ^ info[2]
        a, b = (move >> 1, move & 1) if half else (move & 1, move >> 1)
        piece = value[p * rows : (p + 1) * rows].astype(low)

        @pl.when(info[1] == half)
        def _():
            keep_ref[(a, b) + entry] = piece

        @pl.when(info[1] != half)
        def _():
            send_ref[(a, b) + entry] = piece


def start_all(copies):
    for copy in copies:
        copy.start()


def wait_all(copies):
    for copy in copies:
        copy.wait()


def attn_own_kernel(info, tokens, weights, bias, qkv, ctx, lse):
    group_forward(tokens[...], weights[...], bias[0], info[0], qkv.at[0], ctx.at[0], lse.at[0])


def attn_own(info, tokens, weights, bias):
    local, seq = weights.shape[0] // 4, tokens.shape[0]
    return pl.pallas_call(
        attn_own_kernel,
        in_specs=[smem()] + [vmem()] * 3,
        out_specs=[vmem()] * 3,
        out_shape=[
            shaped((1, 3 * local, seq), low),
            shaped((1, local, seq), low),
            shaped((1, 8, seq), wide),
        ],
        compiler_params=params(24),
        cost_estimate=cost(4),
        name="attn_own",
    )(info, tokens, weights, bias)


def attn_rest_kernel(info, tokens, bias, *refs):
    qkv, ctx, lse, whole, weights, sems, keep_sem = refs[6:]
    parts = weights.shape[0]
    copies = piece_copies(info, refs[:6], weights, sems)
    start_all(copies)
    wait_all(copies)
    keep = pltpu.make_async_copy(weights.at[pl.ds(1, parts - 1)], whole, keep_sem.at[0])
    keep.start()

    def group(k, _):
        out = k - 1
        group_forward(
            tokens[...], weights[k], bias[k], info[0], qkv.at[out], ctx.at[out], lse.at[out]
        )
        return 0

    lax.fori_loop(1, parts, group, 0)
    keep.wait()


def attn_rest(info, tokens, bias, pieces):
    others, rows, cols = pieces[0].shape
    size, seq = rows * GROUP, tokens.shape[0]
    local = size // 4
    return pl.pallas_call(
        attn_rest_kernel,
        in_specs=[smem()] + [vmem()] * 2 + [hbm()] * 6,
        out_specs=[vmem()] * 3 + [hbm()],
        out_shape=[
            shaped((others, 3 * local, seq), low),
            shaped((others, local, seq), low),
            shaped((others, 8, seq), wide),
            shaped((others, size, cols), low),
        ],
        scratch_shapes=[
            pltpu.VMEM((others + 1, size, cols), low),
            pltpu.SemaphoreType.DMA((GROUP * others,)),
            pltpu.SemaphoreType.DMA((1,)),
        ],
        compiler_params=params(32),
        cost_estimate=cost(11),
        name="attn_rest",
    )(info, tokens, bias, *pieces)


def ffn_up_kernel(info, tokens, ctx_own, ctx_rest, bias, vec, out_own, out_rest, up_own, *refs):
    act, slope, skip, normed_ref, hat_ref, inv_ref, whole, out_w, up, sems, own_sems = refs[6:]
    parts, size = up.shape[0], up.shape[1]
    local = size // 4
    tail = pl.ds(3 * local, local)
    out_copies = [pltpu.make_async_copy(out_own.at[tail], out_w.at[0], own_sems.at[1])]
    for k in range(1, parts):
        out_copies.append(
            pltpu.make_async_copy(out_rest.at[k - 1, tail], out_w.at[k], own_sems.at[1 + k])
        )
    start_all(out_copies)
    copies = piece_copies(info, refs[:6], up, sems)
    copies.append(pltpu.make_async_copy(up_own, up.at[0], own_sems.at[0]))
    start_all(copies)
    rows = vec[...]
    b_out, gain_one, bias_one, b_down = (rows[i : i + 1] for i in range(4))
    wait_all(out_copies)
    attended = mm(ctx_own[0], out_w[0], 0, 0)
    for k in range(1, parts):
        attended = attended + mm(ctx_rest[k - 1], out_w[k], 0, 0)
    hat, inv = norm_parts(tokens[...].astype(wide) + attended + b_out)
    hat_ref[...] = hat
    inv_ref[...] = jnp.broadcast_to(inv, inv_ref.shape)
    normed = hat * gain_one + bias_one
    normed_ref[...] = normed.astype(low)
    skip[...] = normed + b_down
    wait_all(copies)
    keep = pltpu.make_async_copy(up, whole, own_sems.at[0])
    keep.start()

    def forward(k, _):
        preact = mm(normed_ref[...], up[k], 1, 0) + bias[k][:, 2 * local :].astype(wide)
        value, derivative = gelu_parts(preact)
        act[k] = value.astype(low)
        slope[k] = derivative.astype(low)
        return 0

    lax.fori_loop(0, parts, forward, 0)
    keep.wait()


def ffn_up(info, tokens, ctx_own, ctx_rest, bias, vec, out_own, out_rest, up_own, pieces):
    seq, width = tokens.shape
    parts, size = ctx_rest.shape[0] + 1, up_own.shape[1]
    return pl.pallas_call(
        ffn_up_kernel,
        in_specs=[smem()] + [vmem()] * 5 + [hbm()] * (3 + 6),
        out_specs=[vmem()] * 6 + [hbm()],
        out_shape=[
            shaped((parts, seq, size), low),
            shaped((parts, seq, size), low),
            shaped((seq, width), wide),
            shaped((seq, width), low),
            shaped((seq, width), wide),
            shaped((seq, 128), wide),
            shaped((parts, width, size), low),
        ],
        scratch_shapes=[
            pltpu.VMEM((parts, ctx_own.shape[1], width), low),
            pltpu.VMEM((parts, width, size), low),
            pltpu.SemaphoreType.DMA((GROUP * (parts - 1),)),
            pltpu.SemaphoreType.DMA((1 + parts,)),
        ],
        compiler_params=params(40),
        cost_estimate=cost(15),
        name="ffn_up",
    )(info, tokens, ctx_own, ctx_rest, bias, vec, out_own, out_rest, up_own, *pieces)


def ffn_down_kernel(info, act, skip, vec, cot, down_own, *refs):
    out, grad_ref, branch_ref, keep, send, small, whole, down, sems, own_sems = refs[6:]
    parts = down.shape[0]
    copies = piece_copies(info, refs[:6], down, sems)
    copies.append(pltpu.make_async_copy(down_own, down.at[0], own_sems.at[0]))
    start_all(copies)
    wait_all(copies)
    hold = pltpu.make_async_copy(down, whole, own_sems.at[0])
    hold.start()
    total = skip[...]
    for k in range(parts):
        total = total + mm(act[k], down[k], 1, 0)
    gain_two, bias_two = vec[4:5], vec[5:6]
    hat_two, inv_two = norm_parts(total)
    out[...] = (hat_two * gain_two + bias_two).astype(low)
    grad = cot[...].astype(wide)
    grad_branch = norm_back(grad * gain_two, hat_two, inv_two)
    grad_ref[...] = grad_branch
    branch_low = grad_branch.astype(low)
    branch_ref[...] = branch_low

    def weight(k, _):
        place_pieces(info, mm(act[k], branch_low, 0, 0), keep, send, (k >> 1, k & 1))
        return 0

    lax.fori_loop(0, parts, weight, 0)
    small[...] = jnp.zeros(small.shape, wide)
    small[3:4] = jnp.sum(grad_branch, axis=0, keepdims=True)
    small[4:5] = jnp.sum(grad * hat_two, axis=0, keepdims=True)
    small[5:6] = jnp.sum(grad, axis=0, keepdims=True)
    hold.wait()


def halves_of(parts, rows, cols):
    return shaped((2, 2, 2, parts // 2, rows // GROUP, cols), low)


def ffn_down(info, act, skip, vec, cot, down_own, pieces):
    parts, seq, size = act.shape
    width = skip.shape[1]
    return pl.pallas_call(
        ffn_down_kernel,
        in_specs=[smem()] + [vmem()] * 4 + [hbm()] * (1 + 6),
        out_specs=[vmem()] * 6 + [hbm()],
        out_shape=[
            shaped((seq, width), low),
            shaped((seq, width), wide),
            shaped((seq, width), low),
            halves_of(parts, size, width),
            halves_of(parts, size, width),
            shaped((16, width), wide),
            shaped((parts, size, width), low),
        ],
        scratch_shapes=[
            pltpu.VMEM((parts, size, width), low),
            pltpu.SemaphoreType.DMA((GROUP * (parts - 1),)),
            pltpu.SemaphoreType.DMA((1,)),
        ],
        compiler_params=params(40),
        cost_estimate=cost(12),
        name="ffn_down",
    )(info, act, skip, vec, cot, down_own, *pieces)


def ffn_back_kernel(
    info, branch_low, grad_branch, slope, normed_low, hat_ref, inv_ref, vec, small_in, up, down,
    keep, send, grad_ref, residual_ref, small, turned, total,
):
    parts = up.shape[0]
    index = lax.broadcasted_iota(jnp.int32, small.shape, 0)

    def put(row, value):
        small[...] = jnp.where(index == row, value, small[...])

    small[...] = small_in[...]
    total[...] = grad_branch[...]
    turned[...] = normed_low[...].T

    def backward(k, _):
        grad_pre = (mm(branch_low[...], down[k], 1, 1) * slope[k].astype(wide)).astype(low)
        put(6 + (info[3] ^ k), jnp.sum(grad_pre.astype(wide), axis=0, keepdims=True))
        place_pieces(info, mm(turned[...], grad_pre, 1, 0), keep, send, (k >> 1, k & 1))
        total[...] += mm(grad_pre, up[k], 1, 1)
        return 0

    lax.fori_loop(0, parts, backward, 0)
    grad_normed = total[...]
    hat = hat_ref[...]
    grad_residual = norm_back(grad_normed * vec[1:2], hat, inv_ref[:, :1])
    grad_ref[...] = grad_residual
    residual_ref[...] = grad_residual.astype(low)
    small[0:1] = jnp.sum(grad_residual, axis=0, keepdims=True)
    small[1:2] = jnp.sum(grad_normed * hat, axis=0, keepdims=True)
    small[2:3] = jnp.sum(grad_normed, axis=0, keepdims=True)


def ffn_back(info, branch_low, grad_branch, slope, normed_low, hat, inv, vec, small, up, down):
    parts, width, size = up.shape
    seq = hat.shape[0]
    return pl.pallas_call(
        ffn_back_kernel,
        in_specs=[smem()] + [vmem()] * 10,
        out_specs=[vmem()] * 5,
        out_shape=[
            halves_of(parts, width, size),
            halves_of(parts, width, size),
            shaped((seq, width), wide),
            shaped((seq, width), low),
            shaped((16, width), wide),
        ],
        scratch_shapes=[pltpu.VMEM((width, seq), low), pltpu.VMEM((seq, width), wide)],
        compiler_params=params(48),
        cost_estimate=cost(15),
        name="ffn_back",
    )(info, branch_low, grad_branch, slope, normed_low, hat, inv, vec, small, up, down)


def attn_back_kernel(first, info, tokens, residual_low, small_in, *refs):
    groups = (refs[:4], refs[4:8])
    keep, send, small, joint = refs[8:]
    local = groups[0][2].shape[1]
    seq, width = tokens.shape
    scale = HD**-0.5
    index = lax.broadcasted_iota(jnp.int32, small.shape, 0)
    small[...] = small_in[...]
    key_pad, query_pad = masked_pad(info[0], seq)
    ones = jnp.ones((8, seq), low)
    for i, (weights, qkv, ctx, lse) in enumerate(groups):
        grad_ctx = mm(weights[0, 3 * local :], residual_low[...], 1, 1).astype(low)
        for h in range(local // HD):
            lo, hi = h * HD, (h + 1) * HD
            query = qkv[0, lo:hi]
            key = qkv[0, local + lo : local + hi]
            value = qkv[0, 2 * local + lo : 2 * local + hi]
            grad_head = grad_ctx[lo:hi]
            scores = mm(
                jnp.concatenate([key, key_pad], 0), jnp.concatenate([query, query_pad], 0), 0, 0
            )
            probs = jnp.exp2(scores * (scale * LOG2E) - lse[0, h : h + 1])
            grad_probs = mm(value, grad_head, 0, 0)
            product = probs * grad_probs
            grad_scores = (product - probs * jnp.sum(product, axis=0, keepdims=True)).astype(low)
            joint[i, lo:hi] = (mm(key, grad_scores, 1, 0) * scale).astype(low)
            joint[i, local + lo : local + hi] = (mm(query, grad_scores, 1, 1) * scale).astype(low)
            joint[i, 2 * local + lo : 2 * local + hi] = mm(
                grad_head, probs.astype(low), 1, 1
            ).astype(low)
        grads = joint[i]
        sums = mm(ones, grads, 1, 1)[:1]
        gap = jnp.zeros((1, 256 - local), wide)
        rest = jnp.zeros((1, width - 512), wide)
        sums = jnp.concatenate([sums[:, :local], gap, sums[:, 2 * local :], gap, rest], 1)
        small[...] = jnp.where(index == 10 + (info[3] ^ (first + i)), sums, small[...])
        shares = jnp.concatenate(
            [mm(grads, tokens[...], 1, 0), mm(ctx[0], residual_low[...], 1, 0)], 0
        )
        place_pieces(info, shares, keep, send, (i,))


def attn_back(first, info, tokens, residual_low, small, own_w, own, rest):
    seq, width = tokens.shape
    size = own_w.shape[1]
    local = size // 4
    specs, arrays = [], []
    for k in (first, first + 1):
        source = (own_w,) + tuple(own) if k == 0 else (rest[3],) + tuple(rest[:3])
        index = (max(k - 1, 0), 0, 0)
        specs += [block((1,) + array.shape[1:], index) for array in source]
        arrays += source
    half = shaped((2, 2, 2, size // GROUP, width), low)
    whole = block((seq, width), (0, 0))
    return pl.pallas_call(
        partial(attn_back_kernel, first),
        grid=(1,),
        in_specs=[smem(), whole, whole, block((16, width), (0, 0))] + specs,
        out_specs=[
            block(half.shape, (0,) * 5),
            block(half.shape, (0,) * 5),
            block((16, width), (0, 0)),
            block((2, 3 * local, seq), (0, 0, 0)),
        ],
        out_shape=[half, half, shaped((16, width), wide), shaped((2, 3 * local, seq), low)],
        compiler_params=params(40),
        cost_estimate=cost(14),
        name="attn_back",
    )(info, tokens, residual_low, small, *arrays)


def grad_tokens_kernel(grad, joint_a, joint_b, own_w, rest_w, out):
    rows = joint_a.shape[1]
    total = grad[...]
    for k in range(4):
        joint = joint_a[k] if k < 2 else joint_b[k - 2]
        weights = own_w[0, :rows] if k == 0 else rest_w[k - 1, :rows]
        total = total + mm(joint, weights, 0, 0)
    out[...] = total.astype(low)


def grad_tokens_of(grad, joint_a, joint_b, own_w, rest_w):
    return pl.pallas_call(
        grad_tokens_kernel,
        in_specs=[vmem()] * 5,
        out_specs=vmem(),
        out_shape=shaped(grad.shape, low),
        compiler_params=params(32),
        cost_estimate=cost(5),
        name="grad_tokens",
    )(grad, joint_a, joint_b, own_w, rest_w)


def gather_rows(info, refs, target):
    for s in range(2):
        first, second, third = refs[3 * s : 3 * s + 3]
        holder = info[1] ^ s
        rows = first.shape[0]
        moves = (0, 1 + holder, 2 - holder, 3)
        for move, view in zip(moves, (first, second, third.at[0], third.at[1])):
            start = pl.multiple_of((holder * 4 + (info[2] ^ move)) * rows, rows)
            target[pl.ds(start, rows), :] = view[...].astype(wide)


def finish_ffn_kernel(info, *refs):
    gather_rows(info, refs[:6], refs[6])


def finish_ffn(info, pieces):
    rows, cols = pieces[0].shape
    return pl.pallas_call(
        finish_ffn_kernel,
        in_specs=[smem()] + [vmem()] * 6,
        out_specs=vmem(),
        out_shape=shaped((GROUP * rows, cols), wide),
        compiler_params=params(16),
        cost_estimate=cost(2),
        name="finish_ffn",
    )(info, *pieces)


def finish_attn_kernel(info, *refs):
    query, key, value, out, whole = refs[6:]
    gather_rows(info, refs[:6], whole)
    local = whole.shape[0] // 4
    query[...] = whole[:local].T
    key[...] = whole[local : 2 * local].T
    value[...] = whole[2 * local : 3 * local].T
    out[...] = whole[3 * local :]


def finish_attn(info, pieces):
    rows, cols = pieces[0].shape
    size = GROUP * rows
    local = size // 4
    return pl.pallas_call(
        finish_attn_kernel,
        in_specs=[smem()] + [vmem()] * 6,
        out_specs=[vmem()] * 4,
        out_shape=[shaped((cols, local), wide)] * 3 + [shaped((local, cols), wide)],
        scratch_shapes=[pltpu.VMEM((size, cols), wide)],
        compiler_params=params(24),
        cost_estimate=cost(2),
        name="finish_attn",
    )(info, *pieces)


class Links:
    def __init__(self, dp_size, parts):
        self.dp_size, self.parts = dp_size, parts

    def move(self, array, partner):
        pairs = []
        for d in range(self.dp_size):
            for t in range(self.parts):
                to_d, to_t = partner(d, t)
                pairs.append((d * self.parts + t, to_d * self.parts + to_t))
        return lax.ppermute(array, ("dp", "tensor"), pairs)

    def bit(self, array, bit):
        return self.move(array, lambda d, t: (d ^ bit, t))

    def core(self, array):
        return self.bit(array, 1)

    def plane(self, array, step):
        return self.move(array, lambda d, t: (d ^ (2 if (d & 1) == step else 4), t))

    def line(self, array, step):
        return self.move(array, lambda d, t: (d, t ^ (1 if (d & 1) == step else 2)))


def add(left, right):
    return (left.astype(wide) + right.astype(wide)).astype(low)


def after(*values):
    return lax.optimization_barrier(values)


class Sum:
    def __init__(self, links, is_odd):
        self.links, self.is_odd = links, is_odd

    def split(self, both):
        return jnp.where(self.is_odd, both[:, 1], both[1]), jnp.where(self.is_odd, both[:, 0], both[0])


def per_device(
    dp_size,
    parts,
    tokens,
    page_lengths,
    w_query,
    b_query,
    w_key,
    w_value,
    b_value,
    w_out,
    b_out,
    ln1_gain,
    ln1_bias,
    w_up,
    b_up,
    w_down,
    b_down,
    ln2_gain,
    ln2_bias,
    cotangent,
):
    links = Links(dp_size, parts)
    me = lax.axis_index("tensor")
    place = lax.axis_index("dp") % GROUP
    core, quarter = place & 1, place >> 1
    is_odd = core == 1
    width = tokens.shape[1]
    local = w_query.shape[1]
    rows = width // GROUP
    length = lax.dynamic_slice_in_dim(page_lengths, me, 1, 0)
    info = jnp.concatenate([length, jnp.stack([core, quarter, me]).astype(jnp.int32)])
    attn_w = jnp.concatenate([w_query.T, w_key.T, w_value.T, w_out], axis=0)
    cut = partial(
        lax.dynamic_slice_in_dim, start_index=(core * 4 + quarter) * rows, slice_size=rows, axis=0
    )
    bias_own = jnp.concatenate([b_query, b_value, b_up])
    bias_rows = jnp.pad(bias_own, (0, 16 * width - bias_own.size)).reshape(16, width)
    vec = jnp.stack([b_out, ln1_gain, ln1_bias, b_down, ln2_gain, ln2_bias, b_down, b_down])
    vec = vec.astype(wide)
    attn_w3 = attn_w[None]

    a0 = jnp.concatenate([cut(attn_w), bias_rows], axis=0)
    u0, d0 = cut(w_up), cut(w_down)
    a1 = links.line(a0, 0)
    a1, u0, tokens_in = after(a1, u0, tokens)
    a2 = links.line(jnp.stack([a0, a1]), 1)
    u1 = links.line(u0, 0)
    own = attn_own(info, tokens_in, attn_w, bias_own.astype(wide)[None, None])
    a2, u1, d0 = after(a2, u1, d0)
    a3 = jnp.concatenate([a1[None], a2])
    bias_rest = a3[:, rows:].reshape(parts - 1, 16 * width)[:, : bias_own.size]
    near, far = bias_rest[0], bias_rest[1]
    bias = jnp.stack(
        [bias_own, jnp.where(is_odd, far, near), jnp.where(is_odd, near, far), bias_rest[2]]
    )
    bias = bias.astype(wide)[:, None]
    a3 = a3[:, :rows]
    a4 = links.plane(a3, 0)
    u2 = links.line(jnp.stack([u0, u1]), 1)
    d1 = links.line(d0, 0)
    a4, u2, d1 = after(a4, u2, d1)
    u3 = jnp.concatenate([u1[None], u2])
    a5 = links.plane(jnp.stack([a3, a4]), 1)
    u4 = links.plane(u3, 0)
    d2 = links.line(jnp.stack([d0, d1]), 1)
    a5, u4, d2 = after(a5, u4, d2)
    d3 = jnp.concatenate([d1[None], d2])
    pieces_a = [a3, a4, a5] + [links.core(array) for array in (a3, a4, a5)]
    u5 = links.plane(jnp.stack([u3, u4]), 1)
    d4 = links.plane(d3, 0)
    rest = attn_rest(info, tokens, bias, pieces_a)
    u5, d4, *rest = after(u5, d4, *rest)
    pieces_u = [u3, u4, u5] + [links.core(array) for array in (u3, u4, u5)]
    d5 = links.plane(jnp.stack([d3, d4]), 1)
    act, slope, skip, normed_low, hat, inv, up = ffn_up(
        info, tokens, own[1], rest[1], bias, vec, attn_w, rest[3], w_up, pieces_u
    )
    d5, act = after(d5, act)
    pieces_d = [d3, d4, d5] + [links.core(array) for array in (d3, d4, d5)]
    output, grad_branch, branch_low, keep_d, send_d, small, down = ffn_down(
        info, act, skip, vec, cotangent, w_down, pieces_d
    )

    line_split = Sum(links, is_odd).split

    def plane_a(keep, got):
        return links.plane(add(keep[1], got[1]), 0), add(keep[0], got[0])

    def plane_b(kept, got):
        return links.plane(add(kept[1], got[1]), 1), add(kept[0], got[0])

    def line_a(kept, got):
        sent, held = line_split(add(kept, got))
        return links.line(sent, 1), held

    def line_b(kept, got):
        both = add(kept, got)
        return links.line(both[1], 0), both[0]

    def settle(kept, got):
        total = kept.astype(wide) + got.astype(wide)
        bit = GROUP
        while bit < dp_size:
            total = total + links.bit(total, bit)
            bit *= 2
        return total.astype(low)

    got_d = links.core(send_d)
    got_d, branch_low = after(got_d, branch_low)
    near_d, kept_d = plane_a(keep_d, got_d)
    keep_u, send_u, grad_residual, residual_low, small = ffn_back(
        info, branch_low, grad_branch, slope, normed_low, hat, inv, vec, small, up, down
    )
    near_d, send_u = after(near_d, send_u)
    got_u = links.core(send_u)
    far_d, kept_d = plane_b(kept_d, near_d)
    far_d, got_u, residual_low = after(far_d, got_u, residual_low)
    near_u, kept_u = plane_a(keep_u, got_u)
    line_d, kept_d = line_a(kept_d, far_d)
    keep_a, send_a, small, joint_a = attn_back(
        0, info, tokens, residual_low, small, attn_w3, own, rest
    )
    near_u, line_d, send_a, small = after(near_u, line_d, send_a, small)
    far_u, kept_u = plane_b(kept_u, near_u)
    last_d, kept_d = line_b(kept_d, line_d)
    got_a = links.core(send_a)
    keep_b, send_b, small, joint_b = attn_back(
        2, info, tokens, residual_low, small, attn_w3, own, rest
    )
    far_u, last_d, got_a, send_b = after(far_u, last_d, got_a, send_b)
    got_b = links.core(send_b)
    line_u, kept_u = line_a(kept_u, far_u)
    sum_d = settle(kept_d, last_d)
    g1 = links.plane(sum_d, 0)
    got_b, line_u, g1, joint_b = after(got_b, line_u, g1, joint_b)
    keep = jnp.stack([keep_a, keep_b], axis=2)
    got = jnp.stack([got_a, got_b], axis=2)
    near_a, kept_a = plane_a(keep, got)
    last_u, kept_u = line_b(kept_u, line_u)
    g2 = links.plane(jnp.stack([sum_d, g1]), 1)
    grad_tokens = grad_tokens_of(grad_residual, joint_a, joint_b, attn_w3, rest[3])
    near_a, last_u, g2, grad_tokens, small = after(near_a, last_u, g2, grad_tokens, small)
    far_a, kept_a = plane_b(kept_a, near_a)
    sum_u = settle(kept_u, last_u)
    h1 = links.plane(sum_u, 0)
    held = [sum_d, g1, g2]
    pieces = held + [links.core(array) for array in held]
    small = small + links.core(small)
    small_got = links.plane(small, 0)
    far_a, h1, small_got, *pieces = after(far_a, h1, small_got, *pieces)
    line, kept_a = line_a(kept_a, far_a)
    h2 = links.plane(jnp.stack([sum_u, h1]), 1)
    small = small + small_got
    small_got = links.plane(small, 1)
    grad_w_down = finish_ffn(info, pieces)
    line, h2, small_got = after(line, h2, small_got)
    last_a, kept_a = line_b(kept_a, line)
    held = [sum_u, h1, h2]
    pieces = held + [links.core(array) for array in held]
    small = small + small_got
    small_got = links.line(small, 0)
    last_a, small_got, *pieces = after(last_a, small_got, *pieces)
    sum_a = settle(kept_a, last_a)
    i1 = links.plane(sum_a, 0)
    small = small + small_got
    small_got = links.line(small, 1)
    grad_w_up = finish_ffn(info, pieces)
    i1, small_got, grad_w_up = after(i1, small_got, grad_w_up)
    small = small + small_got
    bit = GROUP
    while bit < dp_size:
        small = small + links.bit(small, bit)
        bit *= 2
    i2 = links.plane(jnp.stack([sum_a, i1]), 1)
    held = [sum_a, i1, i2]
    pieces = held + [links.core(array) for array in held]
    grad_w_query, grad_w_key, grad_w_value, grad_w_out = finish_attn(info, pieces)
    pair = lax.dynamic_index_in_dim(small, 10 + me, 0, keepdims=False)
    grad_b_up = lax.dynamic_index_in_dim(small, 6 + me, 0, keepdims=False)
    return (
        output,
        grad_tokens,
        grad_w_query,
        pair[:local],
        grad_w_key,
        grad_w_value,
        pair[256 : 256 + local],
        grad_w_out,
        small[0],
        small[1],
        small[2],
        grad_w_up,
        grad_b_up,
        grad_w_down,
        small[3],
        small[4],
        small[5],
    )


def solution(mesh):
    columns, rows, both = P(None, "tensor"), P("tensor", None), P(("dp", "tensor"), None)
    share = P("tensor")
    return jax.shard_map(
        partial(per_device, mesh.shape["dp"], mesh.shape["tensor"]),
        mesh=mesh,
        in_specs=(
            both,
            P("dp"),
            columns,
            share,
            columns,
            columns,
            share,
            rows,
            P(),
            P(),
            P(),
            columns,
            share,
            rows,
            P(),
            P(),
            P(),
            both,
        ),
        out_specs=(
            both,
            both,
            columns,
            share,
            columns,
            columns,
            share,
            rows,
            P(),
            P(),
            P(),
            columns,
            share,
            rows,
            P(),
            P(),
            P(),
        ),
        check_vma=False,
    )
```

time: 391 us -> 275 us (0.70)
  the two profiles are of different devices: /device:TPU:13 before, /device:TPU:0 now
where the time goes in v2:
time: 275 us; the launch traced here: 272 us
  waiting for transfers between devices  103 us (37%)
  Pallas kernels  92.6 us (34%)
  starting transfers between devices  43.9 us (16%)
  local copies, waits for them, and re-layouts  17 us (6%)
  other arithmetic  13.4 us (5%)
    ppermute x57, waiting for transfers between devices, move(): return lax.ppermute(array, ('dp', 'tensor'), pairs)  103 us
    ppermute x57, starting transfers between devices, move(): return lax.ppermute(array, ('dp', 'tensor'), pairs)  43.9 us
    pallas_call x1, Pallas kernels, ffn_back(): pl.pallas_call(ffn_back_kernel, in_specs=[smem()] + [vmem()] * 10, out_sp...  18.5 us
    pallas_call x2, Pallas kernels, attn_back(): pl.pallas_call(partial(attn_back_kernel, first), grid=(1,), in_specs=[sme...  17.9 us
    pallas_call x1, Pallas kernels, ffn_down(): pl.pallas_call(ffn_down_kernel, in_specs=[smem()] + [vmem()] * 4 + [hbm()...  16.4 us
    pallas_call x1, Pallas kernels, ffn_up(): pl.pallas_call(ffn_up_kernel, in_specs=[smem()] + [vmem()] * 5 + [hbm()]...  15.5 us
    pallas_call x1, Pallas kernels, attn_rest(): pl.pallas_call(attn_rest_kernel, in_specs=[smem()] + [vmem()] * 2 + [hbm(...  11.4 us
    unnamed x74, local copies, waits for them, and re-layouts  10.9 us
  transfers between devices with their start and end apart: 57, of which 28 were waited for; matrix products, arithmetic and copies ran while one was open for 4% of the time, Pallas kernels for 27%

profile of v2, /device:TPU:0, one launch (start us, length us, event | category | flops | bytes accessed | tf_op | source)
XLA Modules:
  0.0 272.0 jit_solution(17265974942759843816)
XLA Ops:
  0.7 2.1 concatenate.45
  2.8 1.4 fusion.36
  4.3 3.1 %collective-permute-start = (bf16[112,768]{1,0:T(8,128)(2,1)S(1)}, bf16[112,768]{1,0:T(8,128)(2,1)S(1)}, u32[]{:S(2)}, u32[]{:S(2)}) collective-permute-start(bf16[112,768]{1,0:T(8,128)(2,1)S(1)} %get-tuple-element.264), channel_id=1, source_target_pairs={{0,1},{1,0},{2,3},{3,2},{4,6},{5,7},{6,4},{7,5},{8,9},{9,8},{10,11... | collective-permute-start | bytes 516104 | tf_op jit(solution)/shard_map/ppermute | solution.py:586
  8.3 3.9 %collective-permute-done = bf16[112,768]{1,0:T(8,128)(2,1)S(1)} collective-permute-done((bf16[112,768]{1,0:T(8,128)(2,1)S(1)}, bf16[112,768]{1,0:T(8,128)(2,1)S(1)}, u32[]{:S(2)}, u32[]{:S(2)}) %collective-permute-start) | collective-permute-done | bytes 172064 | tf_op jit(solution)/shard_map/ppermute | solution.py:586
  12.3 2.4 collective-permute-start.1
  14.6 2.6 collective-permute-start.2
  18.1 6.2 %collective-permute-done.2 = bf16[96,768]{1,0:T(8,128)(2,1)S(1)} collective-permute-done((bf16[96,768]{1,0:T(8,128)(2,1)S(1)}, bf16[96,768]{1,0:T(8,128)(2,1)S(1)}, u32[]{:S(2)}, u32[]{:S(2)}) %collective-permute-start.2) | collective-permute-done | bytes 147488 | tf_op jit(solution)/shard_map/ppermute | solution.py:586
  24.4 3.0 %collective-permute-done.1 = bf16[2,112,768]{2,1,0:T(8,128)(2,1)S(1)} collective-permute-done((bf16[2,112,768]{2,1,0:T(8,128)(2,1)S(1)}, bf16[2,112,768]{2,1,0:T(8,128)(2,1)S(1)}, u32[]{:S(2)}, u32[]{:S(2)}) %collective-permute-start.1) | collective-permute-done | bytes 344096 | tf_op jit(solution)/shard_map/ppermute | solution.py:586
  28.2 1.9 collective-permute-start.3
  30.8 2.6 collective-permute-start.5
  33.5 5.2 %collective-permute-done.5 = bf16[96,768]{1,0:T(8,128)(2,1)S(1)} collective-permute-done((bf16[96,768]{1,0:T(8,128)(2,1)S(1)}, bf16[96,768]{1,0:T(8,128)(2,1)S(1)}, u32[]{:S(2)}, u32[]{:S(2)}) %collective-permute-start.5) | collective-permute-done | bytes 147488 | tf_op jit(solution)/shard_map/ppermute | solution.py:586
  38.7 3.1 %collective-permute-done.4 = bf16[2,96,768]{2,1,0:T(8,128)(2,1)S(1)} collective-permute-done((bf16[2,96,768]{2,1,0:T(8,128)(2,1)S(1)}, bf16[2,96,768]{2,1,0:T(8,128)(2,1)S(1)}, u32[]{:S(2)}, u32[]{:S(2)}) %collective-permute-start.4) | collective-permute-done | bytes 294944 | tf_op jit(solution)/shard_map/ppermute | solution.py:586
  41.9 2.0 pad_maximum_fusion.3
  45.2 1.5 collective-permute-start.7
  49.7 8.6 %collective-permute-done.8 = bf16[2,96,768]{2,1,0:T(8,128)(2,1)} collective-permute-done((bf16[2,96,768]{2,1,0:T(8,128)(2,1)}, bf16[2,96,768]{2,1,0:T(8,128)(2,1)}, u32[]{:S(2)}, u32[]{:S(2)}) %collective-permute-start.8) | collective-permute-done | bytes 294944 | tf_op jit(solution)/shard_map/ppermute | solution.py:586
  58.3 2.1 collective-permute-done.6.refs_2_
  61.0 1.8 fusion.34
  64.2 11.4 %attn_rest.1 = (bf16[3,576,512]{2,1,0:T(8,128)(2,1)S(1)}, bf16[3,192,512]{2,1,0:T(8,128)(2,1)S(1)}, f32[3,8,512]{2,1,0:T(8,128)S(1)}, bf16[3,768,768]{2,1,0:T(8,128)(2,1)S(1)}) custom-call(s32[4]{0:T(128)S(1)} %pad_add_fusion.info, bf16[512,768]{1,0:T(8,128)(2,1)S(1)} %copy-done.7, f32[4,1,1152]{2,1,0:T(1,128)S(1)} %maximum_convert_fusion.bias, ...), custom_call_target="tpu_custom_call" | custom-call | flops 12099999744 | bytes 1048576 | tf_op jit(solution)/shard_map/attn_rest/pallas_call | solution.py:222
  75.6 1.9 copy-done.12
  77.5 1.2 copy-done.14
  80.9 1.1 copy-done.8
  82.1 2.9 %attn_own.1 = (bf16[1,576,512]{2,1,0:T(8,128)(2,1)S(1)}, bf16[1,192,512]{2,1,0:T(8,128)(2,1)S(1)}, f32[1,8,512]{2,1,0:T(8,128)S(1)}) custom-call(s32[4]{0:T(128)S(1)} %pad_add_fusion.info, bf16[512,768]{1,0:T(8,128)(2,1)S(1)} %copy-done.8, bf16[768,768]{1,0:T(8,128)(2,1)S(1)} %get-tuple-element.258.weights.out_own, f32[1,1,1152]{2,1,0:T(1,128)S(1)} %convert_element_type.299.bias), custom_call_target="tpu_custom_call" | custom-call | flops 4400000000 | bytes 1048576 | tf_op jit(solution)/shard_map/attn_own/pallas_call | solution.py:183
  85.1 1.1 collective-permute-start.14
  86.4 15.5 %ffn_up.1 = (bf16[4,512,768]{2,1,0:T(8,128)(2,1)}, bf16[4,512,768]{2,1,0:T(8,128)(2,1)}, f32[512,768]{1,0:T(8,128)S(1)}, bf16[512,768]{1,0:T(8,128)(2,1)S(1)}, f...) custom-call(s32[4]{0:T(128)S(1)} %pad_add_fusion.info, ...), custom_call_target="tpu_custom_call" | custom-call | flops 16499999744 | bytes 1048576 | tf_op jit(solution)/shard_map/ffn_up/pallas_call | solution.py:287
  102.9 2.2 collective-permute-done.18.refs_3_
  105.8 16.4 %ffn_down.1 = (bf16[512,768]{1,0:T(8,128)(2,1)}, f32[512,768]{1,0:T(8,128)S(1)}, bf16[512,768]{1,0:T(8,128)(2,1)S(1)}, bf16[2,2,2,2,96,768]{5,4,3,2,1,0:T(8,128)...) custom-call(s32[4]{0:T(128)S(1)} %pad_add_fusion.info, ...), custom_call_target="tpu_custom_call" | custom-call | flops 13200000000 | bytes 1048576 | tf_op jit(solution)/shard_map/ffn_down/pallas_call | solution.py:352
  122.7 4.2 %collective-permute-done.21 = bf16[2,2,2,2,96,768]{5,4,3,2,1,0:T(8,128)(2,1)S(1)} collective-permute-done((bf16[2,2,2,2,96,768]{5,4,3,2,1,0:T(8,128)(2,1)S(1)}, bf16[2,2,2,2,96,768]{5,4,3,2,1,0:T(8,128)(2,1)S(1)}, u32[]{:S(2)}, u32[]{:S(2)}) %collective-permute-start.21) | collective-permute-done | bytes 2359328 | tf_op jit(solution)/shard_map/ppermute | solution.py:586
  127.6 1.7 collective-permute-start.22
  129.2 18.5 %ffn_back.1 = (bf16[2,2,2,2,96,768]{5,4,3,2,1,0:T(8,128)(2,1)}, bf16[2,2,2,2,96,768]{5,4,3,2,1,0:T(8,128)(2,1)}, f32[512,768]{1,0:T(8,128)S(1)}, bf16[512,768]{1,0:T(8,128)(2,1)S(1)}, f32[16,768]{1,0:T(8,128)S(1)}) custom-call(s32[4]{0:T(128)S(1)} %pad_add_fusion.info, bf16[512,768]{1,0:T(8,128)(2,1)S(1)} %get-tuple-element.152.branch_low, ...), custom_call_target="tpu_custom_call" | custom-call | flops 16499999744 | bytes 1048576 | tf_op jit(solution)/shard_map/ffn_back/pallas_call | solution.py:411
  147.9 1.3 collective-permute-start.23
  149.2 8.7 %collective-permute-done.23 = bf16[2,2,96,768]{3,2,1,0:T(8,128)(2,1)S(1)} collective-permute-done((bf16[2,2,96,768]{3,2,1,0:T(8,128)(2,1)S(1)}, bf16[2,2,96,768]{3,2,1,0:T(8,128)(2,1)S(1)}, u32[]{:S(2)}, u32[]{:S(2)}) %collective-permute-start.23) | collective-permute-done | bytes 589856 | tf_op jit(solution)/shard_map/ppermute | solution.py:586
  158.1 1.1 collective-permute-start.26
  160.3 1.4 collective-permute-start.25
  162.2 8.9 %attn_back.2 = (bf16[2,2,2,96,768]{4,3,2,1,0:T(8,128)(2,1)S(1)}, bf16[2,2,2,96,768]{4,3,2,1,0:T(8,128)(2,1)S(1)}, f32[16,768]{1,0:T(8,128)S(1)}, bf16[2,576,512]{2,1,0:T(8,128)(2,1)S(1)}) custom-call(s32[4]{0:T(128)S(1)} %pad_add_fusion.info, bf16[512,768]{1,0:T(8,128)(2,1)S(1)} %copy-done.9, bf16[512,768]{1,0:T(8,128)(2,1)S(1)} %get-tuple-element.165.residual_low, ...), custom_call_target="tpu_custom_call" | custom-call | flops 15399999488 | bytes 1048576 | tf_op jit(solution)/shard_map/attn_back/pallas_call | solution.py:483
  171.1 5.4 %collective-permute-done.25 = bf16[2,2,2,96,768]{4,3,2,1,0:T(8,128)(2,1)S(1)} collective-permute-done((bf16[2,2,2,96,768]{4,3,2,1,0:T(8,128)(2,1)S(1)}, bf16[2,2,2,96,768]{4,3,2,1,0:T(8,128)(2,1)S(1)}, u32[]{:S(2)}, u32[]{:S(2)}) %collective-permute-start.25) | collective-permute-done | bytes 1179680 | tf_op jit(solution)/shard_map/ppermute | solution.py:586
  176.9 1.3 collective-permute-start.27
  178.2 8.9 %attn_back.3 = (bf16[2,2,2,96,768]{4,3,2,1,0:T(8,128)(2,1)S(1)}, bf16[2,2,2,96,768]{4,3,2,1,0:T(8,128)(2,1)S(1)}, f32[16,768]{1,0:T(8,128)S(1)}, bf16[2,576,512]{2,1,0:T(8,128)(2,1)S(1)}) custom-call(s32[4]{0:T(128)S(1)} %pad_add_fusion.info, bf16[512,768]{1,0:T(8,128)(2,1)S(1)} %copy-done.9, bf16[512,768]{1,0:T(8,128)(2,1)S(1)} %get-tuple-element.165.residual_low, ...), custom_call_target="tpu_custom_call" | custom-call | flops 15399999488 | bytes 1048576 | tf_op jit(solution)/shard_map/attn_back/pallas_call | solution.py:483
  188.0 1.7 collective-permute-start.31
  190.4 4.4 %collective-permute-done.32.refs_1_ = bf16[96,768]{1,0:T(8,128)(2,1)S(1)} collective-permute-done((bf16[96,768]{1,0:T(8,128)(2,1)S(1)}, bf16[96,768]{1,0:T(8,128)(2,1)S(1)}, u32[]{:S(2)}, u32[]{:S(2)}) %collective-permute-start.32) | collective-permute-done | bytes 147488 | tf_op jit(solution)/shard_map/ppermute | solution.py:586
  194.9 4.0 %collective-permute-done.31 = bf16[2,96,768]{2,1,0:T(8,128)(2,1)S(1)} collective-permute-done((bf16[2,96,768]{2,1,0:T(8,128)(2,1)S(1)}, bf16[2,96,768]{2,1,0:T(8,128)(2,1)S(1)}, u32[]{:S(2)}, u32[]{:S(2)}) %collective-permute-start.31) | collective-permute-done | bytes 294944 | tf_op jit(solution)/shard_map/ppermute | solution.py:586
  200.3 1.5 collective-permute-start.35
  202.1 3.6 %grad_tokens.1 = bf16[512,768]{1,0:T(8,128)(2,1)} custom-call(f32[512,768]{1,0:T(8,128)S(1)} %get-tuple-element.191.grad, bf16[2,576,512]{2,1,0:T(8,128)(2,1)S(1)} %get-tuple-element.192.joint_a, bf16[2,576,512]{2,1,0:T(8,128)(2,1)S(1)} %get-tuple-element.193.joint_b, bf16[1,768,768]{2,1,0:T(8,128)(2,1)S(1)} %get-tuple-element.257.refs_0_.own_w, ...), custom_call_target="tpu_custom_call" | custom-call | flops 5499999744 | bytes 1048576 | tf_op jit(solution)/shard_map/grad_tokens/pallas_call | solution.py:511
  205.6 1.8 collective-permute-done.34
  207.4 2.9 %collective-permute-done.35.refs_2_ = bf16[2,96,768]{2,1,0:T(8,128)(2,1)S(1)} collective-permute-done((bf16[2,96,768]{2,1,0:T(8,128)(2,1)S(1)}, bf16[2,96,768]{2,1,0:T(8,128)(2,1)S(1)}, u32[]{:S(2)}, u32[]{:S(2)}) %collective-permute-start.35) | collective-permute-done | bytes 294944 | tf_op jit(solution)/shard_map/ppermute | solution.py:586
  210.4 6.3 %collective-permute-done.33 = bf16[2,2,2,96,768]{4,3,2,1,0:T(8,128)(2,1)S(1)} collective-permute-done((bf16[2,2,2,96,768]{4,3,2,1,0:T(8,128)(2,1)S(1)}, bf16[2,2,2,96,768]{4,3,2,1,0:T(8,128)(2,1)S(1)}, u32[]{:S(2)}, u32[]{:S(2)}) %collective-permute-start.33) | collective-permute-done | bytes 1179680 | tf_op jit(solution)/shard_map/ppermute | solution.py:586
  216.8 1.3 collective-permute-start.36
  219.8 1.1 collective-permute-start.37
  221.9 5.4 %collective-permute-done.39 = f32[16,768]{1,0:T(8,128)S(1)} collective-permute-done((f32[16,768]{1,0:T(8,128)S(1)}, f32[16,768]{1,0:T(8,128)S(1)}, u32[]{:S(2)}, u32[]{:S(2)}) %collective-permute-start.39) | collective-permute-done | bytes 49184 | tf_op jit(solution)/shard_map/ppermute | solution.py:586
  227.3 1.5 collective-permute-done.36
  228.9 1.3 collective-permute-start.44
  230.5 1.1 collective-permute-start.45
  232.1 4.1 %collective-permute-done.45 = f32[16,768]{1,0:T(8,128)S(1)} collective-permute-done((f32[16,768]{1,0:T(8,128)S(1)}, f32[16,768]{1,0:T(8,128)S(1)}, u32[]{:S(2)}, u32[]{:S(2)}) %collective-permute-start.45) | collective-permute-done | bytes 49184 | tf_op jit(solution)/shard_map/ppermute | solution.py:586
  236.2 5.0 %collective-permute-done.43 = bf16[2,96,768]{2,1,0:T(8,128)(2,1)S(1)} collective-permute-done((bf16[2,96,768]{2,1,0:T(8,128)(2,1)S(1)}, bf16[2,96,768]{2,1,0:T(8,128)(2,1)S(1)}, u32[]{:S(2)}, u32[]{:S(2)}) %collective-permute-start.43) | collective-permute-done | bytes 294944 | tf_op jit(solution)/shard_map/ppermute | solution.py:586
  241.5 2.0 collective-permute-start.47
  243.5 5.7 %collective-permute-done.47 = f32[16,768]{1,0:T(8,128)S(1)} collective-permute-done((f32[16,768]{1,0:T(8,128)S(1)}, f32[16,768]{1,0:T(8,128)S(1)}, u32[]{:S(2)}, u32[]{:S(2)}) %collective-permute-start.47) | collective-permute-done | bytes 49184 | tf_op jit(solution)/shard_map/ppermute | solution.py:586
  249.4 1.2 collective-permute-start.51
  250.6 2.1 finish_ffn.2
  252.7 1.6 collective-permute-done.52
  255.5 5.9 %collective-permute-done.53.refs_2_ = bf16[2,96,768]{2,1,0:T(8,128)(2,1)S(1)} collective-permute-done((bf16[2,96,768]{2,1,0:T(8,128)(2,1)S(1)}, bf16[2,96,768]{2,1,0:T(8,128)(2,1)S(1)}, u32[]{:S(2)}, u32[]{:S(2)}) %collective-permute-start.53) | collective-permute-done | bytes 294944 | tf_op jit(solution)/shard_map/ppermute | solution.py:586
  261.4 2.1 finish_ffn.3
  266.4 2.1 finish_attn.1
  268.5 1.1 copy.36
  269.6 1.1 copy.37
  270.7 1.1 copy.38
  (203 shorter events, 28.7 us)
Async XLA Ops:
  4.3 7.9 %collective-permute-start = (bf16[112,768]{1,0:T(8,128)(2,1)S(1)}, bf16[112,768]{1,0:T(8,128)(2,1)S(1)}, u32[]{:S(2)}, u32[]{:S(2)}) collective-permute-start(bf16[112,768]{1,0:T(8,128)(2,1)S(1)} %get-tuple-element.264), channel_id=1, source_target_pairs={{0,1},{1,0},{2,3},{3,2},{4,6},{5,7},{6,4},{7,5},{8,9},{9,8},{10,11... | collective-permute-start | bytes 516104 | tf_op jit(solution)/shard_map/ppermute | solution.py:586
  12.3 15.1 %collective-permute-start.1 = (bf16[2,112,768]{2,1,0:T(8,128)(2,1)S(1)}, bf16[2,112,768]{2,1,0:T(8,128)(2,1)S(1)}, u32[]{:S(2)}, u32[]{:S(2)}) collective-permute-start(bf16[2,112,768]{2,1,0:T(8,128)(2,1)S(1)} %pad_maximum_fusion.8), channel_id=1, source_target_pairs={{0,2},{1,3},{2,0},{3,1},{4,5},{5,4},{6,7},{7,6},{8,10},{9,11},{10,... | collective-permute-start | bytes 1032200 | tf_op jit(solution)/shard_map/ppermute | solution.py:586
  14.6 9.7 %collective-permute-start.2 = (bf16[96,768]{1,0:T(8,128)(2,1)S(1)}, bf16[96,768]{1,0:T(8,128)(2,1)S(1)}, u32[]{:S(2)}, u32[]{:S(2)}) collective-permute-start(bf16[96,768]{1,0:T(8,128)(2,1)S(1)} %constant_dynamic-slice_fusion.2), channel_id=1, source_target_pairs={{0,1},{1,0},{2,3},{3,2},{4,6},{5,7},{6,4},{7,5},{8,9},{9,8},{10,11... | collective-permute-start | bytes 442376 | tf_op jit(solution)/shard_map/ppermute | solution.py:586
  28.2 13.6 %collective-permute-start.3 = (bf16[3,96,768]{2,1,0:T(8,128)(2,1)}, bf16[3,96,768]{2,1,0:T(8,128)(2,1)}, u32[]{:S(2)}, u32[]{:S(2)}) collective-permute-start(bf16[3,96,768]{2,1,0:T(8,128)(2,1)} %fusion.20.refs_0_), channel_id=1, source_target_pairs={{0,8},{1,9},{2,10},{3,11},{4,20},{5,21},{6,22},{7,23},{8,0},{9,1},... | collective-permute-start | bytes 1327112 | tf_op jit(solution)/shard_map/ppermute | solution.py:586
  30.2 11.7 %collective-permute-start.4 = (bf16[2,96,768]{2,1,0:T(8,128)(2,1)S(1)}, bf16[2,96,768]{2,1,0:T(8,128)(2,1)S(1)}, u32[]{:S(2)}, u32[]{:S(2)}) collective-permute-start(bf16[2,96,768]{2,1,0:T(8,128)(2,1)S(1)} %pad_maximum_fusion.9), channel_id=1, source_target_pairs={{0,2},{1,3},{2,0},{3,1},{4,5},{5,4},{6,7},{7,6},{8,10},{9,11},{10,... | collective-permute-start | bytes 884744 | tf_op jit(solution)/shard_map/ppermute | solution.py:586
  30.8 7.9 %collective-permute-start.5 = (bf16[96,768]{1,0:T(8,128)(2,1)S(1)}, bf16[96,768]{1,0:T(8,128)(2,1)S(1)}, u32[]{:S(2)}, u32[]{:S(2)}) collective-permute-start(bf16[96,768]{1,0:T(8,128)(2,1)S(1)} %constant_dynamic-slice_fusion.1), channel_id=1, source_target_pairs={{0,1},{1,0},{2,3},{3,2},{4,6},{5,7},{6,4},{7,5},{8,9},{9,8},{10,11... | collective-permute-start | bytes 442376 | tf_op jit(solution)/shard_map/ppermute | solution.py:586
  43.9 16.5 %collective-permute-start.6 = (bf16[2,3,96,768]{3,2,1,0:T(8,128)(2,1)}, bf16[2,3,96,768]{3,2,1,0:T(8,128)(2,1)}, u32[]{:S(2)}, u32[]{:S(2)}) collective-permute-start(bf16[2,3,96,768]{3,2,1,0:T(8,128)(2,1)} %pad_maximum_fusion.3), channel_id=1, source_target_pairs={{0,16},{1,17},{2,18},{3,19},{4,12},{5,13},{6,14},{7,15},{8,24},{9,... | collective-permute-start | bytes 2654216 | tf_op jit(solution)/shard_map/ppermute | solution.py:586
  45.2 17.7 %copy-start = (bf16[3,96,768]{2,1,0:T(8,128)(2,1)}, bf16[3,96,768]{2,1,0:T(8,128)(2,1)S(1)}, u32[]{:S(2)}) copy-start(bf16[3,96,768]{2,1,0:T(8,128)(2,1)S(1)} %get-tuple-element.262.refs_0_) | copy-start | bytes 1327108
  45.2 13.1 %collective-permute-start.7 = (bf16[3,96,768]{2,1,0:T(8,128)(2,1)S(1)}, bf16[3,96,768]{2,1,0:T(8,128)(2,1)S(1)}, u32[]{:S(2)}, u32[]{:S(2)}) collective-permute-start(bf16[3,96,768]{2,1,0:T(8,128)(2,1)S(1)} %get-tuple-element.262.refs_0_), channel_id=1, source_target_pairs={{0,8},{1,9},{2,10},{3,11},{4,20},{5,21},{6,22},{7,23},{8,0},{9,1},... | collective-permute-start | bytes 1327112 | tf_op jit(solution)/shard_map/ppermute | solution.py:586
  47.4 10.9 %collective-permute-start.8 = (bf16[2,96,768]{2,1,0:T(8,128)(2,1)}, bf16[2,96,768]{2,1,0:T(8,128)(2,1)}, u32[]{:S(2)}, u32[]{:S(2)}) collective-permute-start(bf16[2,96,768]{2,1,0:T(8,128)(2,1)} %pad_maximum_fusion.10), channel_id=1, source_target_pairs={{0,2},{1,3},{2,0},{3,1},{4,5},{5,4},{6,7},{7,6},{8,10},{9,11},{10,... | collective-permute-start | bytes 884744 | tf_op jit(solution)/shard_map/ppermute | solution.py:586
  48.8 15.0 %collective-permute-start.11 = (bf16[3,96,768]{2,1,0:T(8,128)(2,1)}, bf16[3,96,768]{2,1,0:T(8,128)(2,1)S(1)}, u32[]{:S(2)}, u32[]{:S(2)}) collective-permute-start(bf16[3,96,768]{2,1,0:T(8,128)(2,1)} %fusion.20.refs_0_), channel_id=1, source_target_pairs={{0,4},{1,5},{2,6},{3,7},{4,0},{5,1},{6,2},{7,3},{8,12},{9,13},{10,... | collective-permute-start | bytes 1327112 | tf_op jit(solution)/shard_map/ppermute | solution.py:586
  60.4 3.4 %collective-permute-start.13 = (bf16[2,3,96,768]{3,2,1,0:T(8,128)(2,1)}, bf16[2,3,96,768]{3,2,1,0:T(8,128)(2,1)S(1)}, u32[]{:S(2)}, u32[]{:S(2)}) collective-permute-start(bf16[2,3,96,768]{3,2,1,0:T(8,128)(2,1)} %collective-permute-done.6.refs_2_), channel_id=1, source_target_pairs={{0,4},{1,5},{2,6},{3,7},{4,0},{5,1},{6,2},{7,3},{8,12},{9,13},{10,... | collective-permute-start | bytes 2654216 | tf_op jit(solution)/shard_map/ppermute | solution.py:586
  60.4 3.3 %collective-permute-start.12 = (bf16[3,96,768]{2,1,0:T(8,128)(2,1)}, bf16[3,96,768]{2,1,0:T(8,128)(2,1)S(1)}, u32[]{:S(2)}, u32[]{:S(2)}) collective-permute-start(bf16[3,96,768]{2,1,0:T(8,128)(2,1)} %collective-permute-done.3.refs_1_), channel_id=1, source_target_pairs={{0,4},{1,5},{2,6},{3,7},{4,0},{5,1},{6,2},{7,3},{8,12},{9,13},{10,... | collective-permute-start | bytes 1327112 | tf_op jit(solution)/shard_map/ppermute | solution.py:586
  62.9 16.7 %collective-permute-start.10 = (bf16[3,96,768]{2,1,0:T(8,128)(2,1)S(1)}, bf16[3,96,768]{2,1,0:T(8,128)(2,1)S(1)}, u32[]{:S(2)}, u32[]{:S(2)}) collective-permute-start(bf16[3,96,768]{2,1,0:T(8,128)(2,1)S(1)} %get-tuple-element.260.refs_0_), channel_id=1, source_target_pairs={{0,8},{1,9},{2,10},{3,11},{4,20},{5,21},{6,22},{7,23},{8,0},{9,1},... | collective-permute-start | bytes 1327112 | tf_op jit(solution)/shard_map/ppermute | solution.py:586
  63.4 16.8 %copy-start.29 = (bf16[768]{0:T(1024)(128)(2,1)S(1)}, bf16[768]{0:T(1024)(128)(2,1)}, u32[]{:S(2)}) copy-start(bf16[768]{0:T(1024)(128)(2,1)} %param.32) | copy-start | bytes 4612
  63.4 16.8 %copy-start.30 = (bf16[768]{0:T(1024)(128)(2,1)S(1)}, bf16[768]{0:T(1024)(128)(2,1)}, u32[]{:S(2)}) copy-start(bf16[768]{0:T(1024)(128)(2,1)} %param.33) | copy-start | bytes 4612
  63.4 16.8 %copy-start.31 = (bf16[768]{0:T(1024)(128)(2,1)S(1)}, bf16[768]{0:T(1024)(128)(2,1)}, u32[]{:S(2)}) copy-start(bf16[768]{0:T(1024)(128)(2,1)} %param.34) | copy-start | bytes 4612
  63.4 16.5 %collective-permute-start.9 = (bf16[2,3,96,768]{3,2,1,0:T(8,128)(2,1)S(1)}, bf16[2,3,96,768]{3,2,1,0:T(8,128)(2,1)}, u32[]{:S(2)}, u32[]{:S(2)}) collective-permute-start(bf16[2,3,96,768]{3,2,1,0:T(8,128)(2,1)S(1)} %pad_maximum_fusion.4), channel_id=1, source_target_pairs={{0,16},{1,17},{2,18},{3,19},{4,12},{5,13},{6,14},{7,15},{8,24},{9,... | collective-permute-start | bytes 2654216 | tf_op jit(solution)/shard_map/ppermute | solution.py:586
  79.9 6.3 %collective-permute-start.17 = (bf16[2,3,96,768]{3,2,1,0:T(8,128)(2,1)}, bf16[2,3,96,768]{3,2,1,0:T(8,128)(2,1)}, u32[]{:S(2)}, u32[]{:S(2)}) collective-permute-start(bf16[2,3,96,768]{3,2,1,0:T(8,128)(2,1)} %collective-permute-done.9.refs_2_), channel_id=1, source_target_pairs={{0,4},{1,5},{2,6},{3,7},{4,0},{5,1},{6,2},{7,3},{8,12},{9,13},{10,... | collective-permute-start | bytes 2654216 | tf_op jit(solution)/shard_map/ppermute | solution.py:586
  80.3 5.9 %collective-permute-start.15 = (bf16[3,96,768]{2,1,0:T(8,128)(2,1)}, bf16[3,96,768]{2,1,0:T(8,128)(2,1)S(1)}, u32[]{:S(2)}, u32[]{:S(2)}) collective-permute-start(bf16[3,96,768]{2,1,0:T(8,128)(2,1)} %copy-done), channel_id=1, source_target_pairs={{0,4},{1,5},{2,6},{3,7},{4,0},{5,1},{6,2},{7,3},{8,12},{9,13},{10,... | collective-permute-start | bytes 1327112 | tf_op jit(solution)/shard_map/ppermute | solution.py:586
  80.8 5.4 %collective-permute-start.16 = (bf16[3,96,768]{2,1,0:T(8,128)(2,1)S(1)}, bf16[3,96,768]{2,1,0:T(8,128)(2,1)S(1)}, u32[]{:S(2)}, u32[]{:S(2)}) collective-permute-start(bf16[3,96,768]{2,1,0:T(8,128)(2,1)S(1)} %collective-permute-done.7.refs_1_), channel_id=1, source_target_pairs={{0,4},{1,5},{2,6},{3,7},{4,0},{5,1},{6,2},{7,3},{8,12},{9,13},{10,... | collective-permute-start | bytes 1327112 | tf_op jit(solution)/shard_map/ppermute | solution.py:586
  85.1 16.8 %collective-permute-start.14 = (bf16[2,3,96,768]{3,2,1,0:T(8,128)(2,1)S(1)}, bf16[2,3,96,768]{3,2,1,0:T(8,128)(2,1)S(1)}, u32[]{:S(2)}, u32[]{:S(2)}) collective-permute-start(bf16[2,3,96,768]{3,2,1,0:T(8,128)(2,1)S(1)} %pad_maximum_fusion.5), channel_id=1, source_target_pairs={{0,16},{1,17},{2,18},{3,19},{4,12},{5,13},{6,14},{7,15},{8,24},{9,... | collective-permute-start | bytes 2654216 | tf_op jit(solution)/shard_map/ppermute | solution.py:586
  86.4 19.3 %copy-start.5 = (bf16[768,768]{1,0:T(8,128)(2,1)S(1)}, bf16[768,768]{1,0:T(8,128)(2,1)}, u32[]{:S(2)}) copy-start(bf16[768,768]{1,0:T(8,128)(2,1)} %down_own.1) | copy-start | bytes 3538948
  86.4 19.3 %copy-start.6 = (bf16[512,768]{1,0:T(8,128)(2,1)S(1)}, bf16[512,768]{1,0:T(8,128)(2,1)}, u32[]{:S(2)}) copy-start(bf16[512,768]{1,0:T(8,128)(2,1)} %cot.1) | copy-start | bytes 2359300
  102.0 20.2 %copy-start.16 = (f32[512,768]{1,0:T(8,128)}, f32[512,768]{1,0:T(8,128)S(1)}, u32[]{:S(2)}) copy-start(f32[512,768]{1,0:T(8,128)S(1)} %get-tuple-element.156.hat_ref) | copy-start | bytes 4718596
  102.0 3.8 %collective-permute-start.20 = (bf16[2,3,96,768]{3,2,1,0:T(8,128)(2,1)S(1)}, bf16[2,3,96,768]{3,2,1,0:T(8,128)(2,1)S(1)}, u32[]{:S(2)}, u32[]{:S(2)}) collective-permute-start(bf16[2,3,96,768]{3,2,1,0:T(8,128)(2,1)S(1)} %collective-permute-done.14.refs_2_), channel_id=1, source_target_pairs={{0,4},{1,5},{2,6},{3,7},{4,0},{5,1},{6,2},{7,3},{8,12},{9,13},{10,... | collective-permute-start | bytes 2654216 | tf_op jit(solution)/shard_map/ppermute | solution.py:586
  102.4 2.7 collective-permute-start.18
  102.6 3.2 %collective-permute-start.19 = (bf16[3,96,768]{2,1,0:T(8,128)(2,1)S(1)}, bf16[3,96,768]{2,1,0:T(8,128)(2,1)S(1)}, u32[]{:S(2)}, u32[]{:S(2)}) collective-permute-start(bf16[3,96,768]{2,1,0:T(8,128)(2,1)S(1)} %collective-permute-done.10.refs_1_), channel_id=1, source_target_pairs={{0,4},{1,5},{2,6},{3,7},{4,0},{5,1},{6,2},{7,3},{8,12},{9,13},{10,... | collective-permute-start | bytes 1327112 | tf_op jit(solution)/shard_map/ppermute | solution.py:586
  122.2 4.6 %collective-permute-start.21 = (bf16[2,2,2,2,96,768]{5,4,3,2,1,0:T(8,128)(2,1)S(1)}, bf16[2,2,2,2,96,768]{5,4,3,2,1,0:T(8,128)(2,1)S(1)}, u32[]{:S(2)}, u32[]{:S(2)}) collective-permute-start(bf16[2,2,2,2,96,768]{5,4,3,2,1,0:T(8,128)(2,1)S(1)} %get-tuple-element.149), channel_id=1, source_target_pairs={{0,4},{1,5},{2,6},{3,7},{4,0},{5,1},{6,2},{7,3},{8,12},{9,13},{10,... | collective-permute-start | bytes 7077896 | tf_op jit(solution)/shard_map/ppermute | solution.py:586
  127.6 20.2 %collective-permute-start.22 = (bf16[2,2,2,96,768]{4,3,2,1,0:T(8,128)(2,1)S(1)}, bf16[2,2,2,96,768]{4,3,2,1,0:T(8,128)(2,1)S(1)}, u32[]{:S(2)}, u32[]{:S(2)}) collective-permute-start(bf16[2,2,2,96,768]{4,3,2,1,0:T(8,128)(2,1)S(1)} %get-tuple-element.255), channel_id=1, source_target_pairs={{0,8},{1,9},{2,10},{3,11},{4,20},{5,21},{6,22},{7,23},{8,0},{9,1},... | collective-permute-start | bytes 3538952 | tf_op jit(solution)/shard_map/ppermute | solution.py:586
  147.8 10.1 %collective-permute-start.24 = (bf16[2,2,2,2,96,768]{5,4,3,2,1,0:T(8,128)(2,1)}, bf16[2,2,2,2,96,768]{5,4,3,2,1,0:T(8,128)(2,1)S(1)}, u32[]{:S(2)}, u32[]{:S(2)}) collective-permute-start(bf16[2,2,2,2,96,768]{5,4,3,2,1,0:T(8,128)(2,1)} %get-tuple-element.163), channel_id=1, source_target_pairs={{0,4},{1,5},{2,6},{3,7},{4,0},{5,1},{6,2},{7,3},{8,12},{9,13},{10,... | collective-permute-start | bytes 7077896 | tf_op jit(solution)/shard_map/ppermute | solution.py:586
  147.9 9.9 %collective-permute-start.23 = (bf16[2,2,96,768]{3,2,1,0:T(8,128)(2,1)S(1)}, bf16[2,2,96,768]{3,2,1,0:T(8,128)(2,1)S(1)}, u32[]{:S(2)}, u32[]{:S(2)}) collective-permute-start(bf16[2,2,96,768]{3,2,1,0:T(8,128)(2,1)S(1)} %fusion.14), channel_id=1, source_target_pairs={{0,16},{1,17},{2,18},{3,19},{4,12},{5,13},{6,14},{7,15},{8,24},{9,... | collective-permute-start | bytes 1769480 | tf_op jit(solution)/shard_map/ppermute | solution.py:586
  158.1 13.0 %collective-permute-start.26 = (bf16[2,96,768]{2,1,0:T(8,128)(2,1)S(1)}, bf16[2,96,768]{2,1,0:T(8,128)(2,1)S(1)}, u32[]{:S(2)}, u32[]{:S(2)}) collective-permute-start(bf16[2,96,768]{2,1,0:T(8,128)(2,1)S(1)} %fusion.26), channel_id=1, source_target_pairs={{0,2},{1,3},{2,0},{3,1},{4,5},{5,4},{6,7},{7,6},{8,10},{9,11},{10,... | collective-permute-start | bytes 884744 | tf_op jit(solution)/shard_map/ppermute | solution.py:586
  160.3 16.3 %collective-permute-start.25 = (bf16[2,2,2,96,768]{4,3,2,1,0:T(8,128)(2,1)S(1)}, bf16[2,2,2,96,768]{4,3,2,1,0:T(8,128)(2,1)S(1)}, u32[]{:S(2)}, u32[]{:S(2)}) collective-permute-start(bf16[2,2,2,96,768]{4,3,2,1,0:T(8,128)(2,1)S(1)} %get-tuple-element.253), channel_id=1, source_target_pairs={{0,8},{1,9},{2,10},{3,11},{4,20},{5,21},{6,22},{7,23},{8,0},{9,1},... | collective-permute-start | bytes 3538952 | tf_op jit(solution)/shard_map/ppermute | solution.py:586
  176.7 10.5 %collective-permute-start.28 = (bf16[96,768]{1,0:T(8,128)(2,1)S(1)}, bf16[96,768]{1,0:T(8,128)(2,1)S(1)}, u32[]{:S(2)}, u32[]{:S(2)}) collective-permute-start(bf16[96,768]{1,0:T(8,128)(2,1)S(1)} %slice_bitcast_fusion.23), channel_id=1, source_target_pairs={{0,1},{1,0},{2,3},{3,2},{4,6},{5,7},{6,4},{7,5},{8,9},{9,8},{10,11... | collective-permute-start | bytes 442376 | tf_op jit(solution)/shard_map/ppermute | solution.py:586
  176.9 10.2 %collective-permute-start.27 = (bf16[2,2,96,768]{3,2,1,0:T(8,128)(2,1)S(1)}, bf16[2,2,96,768]{3,2,1,0:T(8,128)(2,1)S(1)}, u32[]{:S(2)}, u32[]{:S(2)}) collective-permute-start(bf16[2,2,96,768]{3,2,1,0:T(8,128)(2,1)S(1)} %fusion.16), channel_id=1, source_target_pairs={{0,16},{1,17},{2,18},{3,19},{4,12},{5,13},{6,14},{7,15},{8,24},{9,... | collective-permute-start | bytes 1769480 | tf_op jit(solution)/shard_map/ppermute | solution.py:586
  178.2 9.0 %collective-permute-start.29 = (bf16[2,2,2,96,768]{4,3,2,1,0:T(8,128)(2,1)S(1)}, bf16[2,2,2,96,768]{4,3,2,1,0:T(8,128)(2,1)S(1)}, u32[]{:S(2)}, u32[]{:S(2)}) collective-permute-start(bf16[2,2,2,96,768]{4,3,2,1,0:T(8,128)(2,1)S(1)} %get-tuple-element.181), channel_id=1, source_target_pairs={{0,4},{1,5},{2,6},{3,7},{4,0},{5,1},{6,2},{7,3},{8,12},{9,13},{10,... | collective-permute-start | bytes 3538952 | tf_op jit(solution)/shard_map/ppermute | solution.py:586
  187.1 11.7 %collective-permute-start.30 = (bf16[2,2,2,96,768]{4,3,2,1,0:T(8,128)(2,1)S(1)}, bf16[2,2,2,96,768]{4,3,2,1,0:T(8,128)(2,1)S(1)}, u32[]{:S(2)}, u32[]{:S(2)}) collective-permute-start(bf16[2,2,2,96,768]{4,3,2,1,0:T(8,128)(2,1)S(1)} %get-tuple-element.184), channel_id=1, source_target_pairs={{0,4},{1,5},{2,6},{3,7},{4,0},{5,1},{6,2},{7,3},{8,12},{9,13},{10,... | collective-permute-start | bytes 3538952 | tf_op jit(solution)/shard_map/ppermute | solution.py:586
  188.0 10.9 %collective-permute-start.31 = (bf16[2,96,768]{2,1,0:T(8,128)(2,1)S(1)}, bf16[2,96,768]{2,1,0:T(8,128)(2,1)S(1)}, u32[]{:S(2)}, u32[]{:S(2)}) collective-permute-start(bf16[2,96,768]{2,1,0:T(8,128)(2,1)S(1)} %fusion.24), channel_id=1, source_target_pairs={{0,2},{1,3},{2,0},{3,1},{4,5},{5,4},{6,7},{7,6},{8,10},{9,11},{10,... | collective-permute-start | bytes 884744 | tf_op jit(solution)/shard_map/ppermute | solution.py:586
  189.7 5.2 %collective-permute-start.32 = (bf16[96,768]{1,0:T(8,128)(2,1)S(1)}, bf16[96,768]{1,0:T(8,128)(2,1)S(1)}, u32[]{:S(2)}, u32[]{:S(2)}) collective-permute-start(bf16[96,768]{1,0:T(8,128)(2,1)S(1)} %fusion.29.refs_0_), channel_id=1, source_target_pairs={{0,8},{1,9},{2,10},{3,11},{4,20},{5,21},{6,22},{7,23},{8,0},{9,1},... | collective-permute-start | bytes 442376 | tf_op jit(solution)/shard_map/ppermute | solution.py:586
  199.5 17.1 %collective-permute-start.33 = (bf16[2,2,2,96,768]{4,3,2,1,0:T(8,128)(2,1)S(1)}, bf16[2,2,2,96,768]{4,3,2,1,0:T(8,128)(2,1)S(1)}, u32[]{:S(2)}, u32[]{:S(2)}) collective-permute-start(bf16[2,2,2,96,768]{4,3,2,1,0:T(8,128)(2,1)S(1)} %get-tuple-element.252), channel_id=1, source_target_pairs={{0,8},{1,9},{2,10},{3,11},{4,20},{5,21},{6,22},{7,23},{8,0},{9,1},... | collective-permute-start | bytes 3538952 | tf_op jit(solution)/shard_map/ppermute | solution.py:586
  200.3 10.0 %collective-permute-start.35 = (bf16[2,96,768]{2,1,0:T(8,128)(2,1)S(1)}, bf16[2,96,768]{2,1,0:T(8,128)(2,1)S(1)}, u32[]{:S(2)}, u32[]{:S(2)}) collective-permute-start(bf16[2,96,768]{2,1,0:T(8,128)(2,1)S(1)} %pad_maximum_fusion.11), channel_id=1, source_target_pairs={{0,16},{1,17},{2,18},{3,19},{4,12},{5,13},{6,14},{7,15},{8,24},{9,... | collective-permute-start | bytes 884744 | tf_op jit(solution)/shard_map/ppermute | solution.py:586
  201.9 5.5 %collective-permute-start.34 = (bf16[96,768]{1,0:T(8,128)(2,1)S(1)}, bf16[96,768]{1,0:T(8,128)(2,1)S(1)}, u32[]{:S(2)}, u32[]{:S(2)}) collective-permute-start(bf16[96,768]{1,0:T(8,128)(2,1)S(1)} %slice_bitcast_fusion.21), channel_id=1, source_target_pairs={{0,1},{1,0},{2,3},{3,2},{4,6},{5,7},{6,4},{7,5},{8,9},{9,8},{10,11... | collective-permute-start | bytes 442376 | tf_op jit(solution)/shard_map/ppermute | solution.py:586
  216.8 12.1 %collective-permute-start.36 = (bf16[2,2,96,768]{3,2,1,0:T(8,128)(2,1)S(1)}, bf16[2,2,96,768]{3,2,1,0:T(8,128)(2,1)S(1)}, u32[]{:S(2)}, u32[]{:S(2)}) collective-permute-start(bf16[2,2,96,768]{3,2,1,0:T(8,128)(2,1)S(1)} %fusion.19), channel_id=1, source_target_pairs={{0,16},{1,17},{2,18},{3,19},{4,12},{5,13},{6,14},{7,15},{8,24},{9,... | collective-permute-start | bytes 1769480 | tf_op jit(solution)/shard_map/ppermute | solution.py:586
  218.0 2.9 %collective-permute-start.40 = (bf16[96,768]{1,0:T(8,128)(2,1)S(1)}, bf16[96,768]{1,0:T(8,128)(2,1)S(1)}, u32[]{:S(2)}, u32[]{:S(2)}) collective-permute-start(bf16[96,768]{1,0:T(8,128)(2,1)S(1)} %fusion.29.refs_0_), channel_id=1, source_target_pairs={{0,4},{1,5},{2,6},{3,7},{4,0},{5,1},{6,2},{7,3},{8,12},{9,13},{10,... | collective-permute-start | bytes 442376 | tf_op jit(solution)/shard_map/ppermute | solution.py:586
  218.0 3.8 %collective-permute-start.41 = (bf16[96,768]{1,0:T(8,128)(2,1)S(1)}, bf16[96,768]{1,0:T(8,128)(2,1)S(1)}, u32[]{:S(2)}, u32[]{:S(2)}) collective-permute-start(bf16[96,768]{1,0:T(8,128)(2,1)S(1)} %collective-permute-done.32.refs_1_), channel_id=1, source_target_pairs={{0,4},{1,5},{2,6},{3,7},{4,0},{5,1},{6,2},{7,3},{8,12},{9,13},{10,... | collective-permute-start | bytes 442376 | tf_op jit(solution)/shard_map/ppermute | solution.py:586
  218.5 1.2 collective-permute-start.38
  218.6 8.8 %collective-permute-start.42 = (bf16[2,96,768]{2,1,0:T(8,128)(2,1)S(1)}, bf16[2,96,768]{2,1,0:T(8,128)(2,1)S(1)}, u32[]{:S(2)}, u32[]{:S(2)}) collective-permute-start(bf16[2,96,768]{2,1,0:T(8,128)(2,1)S(1)} %collective-permute-done.35.refs_2_), channel_id=1, source_target_pairs={{0,4},{1,5},{2,6},{3,7},{4,0},{5,1},{6,2},{7,3},{8,12},{9,13},{10,... | collective-permute-start | bytes 884744 | tf_op jit(solution)/shard_map/ppermute | solution.py:586
  219.8 7.6 %collective-permute-start.37 = (bf16[96,768]{1,0:T(8,128)(2,1)S(1)}, bf16[96,768]{1,0:T(8,128)(2,1)S(1)}, u32[]{:S(2)}, u32[]{:S(2)}) collective-permute-start(bf16[96,768]{1,0:T(8,128)(2,1)S(1)} %fusion.28.refs_0_), channel_id=1, source_target_pairs={{0,8},{1,9},{2,10},{3,11},{4,20},{5,21},{6,22},{7,23},{8,0},{9,1},... | collective-permute-start | bytes 442376 | tf_op jit(solution)/shard_map/ppermute | solution.py:586
  220.9 6.4 %collective-permute-start.39 = (f32[16,768]{1,0:T(8,128)S(1)}, f32[16,768]{1,0:T(8,128)S(1)}, u32[]{:S(2)}, u32[]{:S(2)}) collective-permute-start(f32[16,768]{1,0:T(8,128)S(1)} %add.140), channel_id=1, source_target_pairs={{0,8},{1,9},{2,10},{3,11},{4,20},{5,21},{6,22},{7,23},{8,0},{9,1},... | collective-permute-start | bytes 147464 | tf_op jit(solution)/shard_map/ppermute | solution.py:586
  228.9 7.3 %collective-permute-start.44 = (bf16[2,96,768]{2,1,0:T(8,128)(2,1)S(1)}, bf16[2,96,768]{2,1,0:T(8,128)(2,1)S(1)}, u32[]{:S(2)}, u32[]{:S(2)}) collective-permute-start(bf16[2,96,768]{2,1,0:T(8,128)(2,1)S(1)} %pad_maximum_fusion.12), channel_id=1, source_target_pairs={{0,16},{1,17},{2,18},{3,19},{4,12},{5,13},{6,14},{7,15},{8,24},{9,... | collective-permute-start | bytes 884744 | tf_op jit(solution)/shard_map/ppermute | solution.py:586
  230.4 10.8 %collective-permute-start.43 = (bf16[2,96,768]{2,1,0:T(8,128)(2,1)S(1)}, bf16[2,96,768]{2,1,0:T(8,128)(2,1)S(1)}, u32[]{:S(2)}, u32[]{:S(2)}) collective-permute-start(bf16[2,96,768]{2,1,0:T(8,128)(2,1)S(1)} %fusion.21), channel_id=1, source_target_pairs={{0,2},{1,3},{2,0},{3,1},{4,5},{5,4},{6,7},{7,6},{8,10},{9,11},{10,... | collective-permute-start | bytes 884744 | tf_op jit(solution)/shard_map/ppermute | solution.py:586
  230.5 5.7 %collective-permute-start.45 = (f32[16,768]{1,0:T(8,128)S(1)}, f32[16,768]{1,0:T(8,128)S(1)}, u32[]{:S(2)}, u32[]{:S(2)}) collective-permute-start(f32[16,768]{1,0:T(8,128)S(1)} %add.142), channel_id=1, source_target_pairs={{0,16},{1,17},{2,18},{3,19},{4,12},{5,13},{6,14},{7,15},{8,24},{9,... | collective-permute-start | bytes 147464 | tf_op jit(solution)/shard_map/ppermute | solution.py:586
  231.6 11.9 %collective-permute-start.48 = (bf16[96,768]{1,0:T(8,128)(2,1)S(1)}, bf16[96,768]{1,0:T(8,128)(2,1)S(1)}, u32[]{:S(2)}, u32[]{:S(2)}) collective-permute-start(bf16[96,768]{1,0:T(8,128)(2,1)S(1)} %fusion.28.refs_0_), channel_id=1, source_target_pairs={{0,4},{1,5},{2,6},{3,7},{4,0},{5,1},{6,2},{7,3},{8,12},{9,13},{10,... | collective-permute-start | bytes 442376 | tf_op jit(solution)/shard_map/ppermute | solution.py:586
  231.6 11.9 %collective-permute-start.49 = (bf16[96,768]{1,0:T(8,128)(2,1)S(1)}, bf16[96,768]{1,0:T(8,128)(2,1)S(1)}, u32[]{:S(2)}, u32[]{:S(2)}) collective-permute-start(bf16[96,768]{1,0:T(8,128)(2,1)S(1)} %collective-permute-done.37.refs_1_), channel_id=1, source_target_pairs={{0,4},{1,5},{2,6},{3,7},{4,0},{5,1},{6,2},{7,3},{8,12},{9,13},{10,... | collective-permute-start | bytes 442376 | tf_op jit(solution)/shard_map/ppermute | solution.py:586
  241.3 7.9 %collective-permute-start.50 = (bf16[2,96,768]{2,1,0:T(8,128)(2,1)S(1)}, bf16[2,96,768]{2,1,0:T(8,128)(2,1)S(1)}, u32[]{:S(2)}, u32[]{:S(2)}) collective-permute-start(bf16[2,96,768]{2,1,0:T(8,128)(2,1)S(1)} %collective-permute-done.44.refs_2_), channel_id=1, source_target_pairs={{0,4},{1,5},{2,6},{3,7},{4,0},{5,1},{6,2},{7,3},{8,12},{9,13},{10,... | collective-permute-start | bytes 884744 | tf_op jit(solution)/shard_map/ppermute | solution.py:586
  241.4 7.8 %collective-permute-start.46 = (bf16[96,768]{1,0:T(8,128)(2,1)S(1)}, bf16[96,768]{1,0:T(8,128)(2,1)S(1)}, u32[]{:S(2)}, u32[]{:S(2)}) collective-permute-start(bf16[96,768]{1,0:T(8,128)(2,1)S(1)} %slice_bitcast_fusion.18), channel_id=1, source_target_pairs={{0,1},{1,0},{2,3},{3,2},{4,6},{5,7},{6,4},{7,5},{8,9},{9,8},{10,11... | collective-permute-start | bytes 442376 | tf_op jit(solution)/shard_map/ppermute | solution.py:586
  241.5 7.7 %collective-permute-start.47 = (f32[16,768]{1,0:T(8,128)S(1)}, f32[16,768]{1,0:T(8,128)S(1)}, u32[]{:S(2)}, u32[]{:S(2)}) collective-permute-start(f32[16,768]{1,0:T(8,128)S(1)} %add.144), channel_id=1, source_target_pairs={{0,1},{1,0},{2,3},{3,2},{4,6},{5,7},{6,4},{7,5},{8,9},{9,8},{10,11... | collective-permute-start | bytes 147464 | tf_op jit(solution)/shard_map/ppermute | solution.py:586
  249.3 5.1 %collective-permute-start.52 = (f32[16,768]{1,0:T(8,128)S(1)}, f32[16,768]{1,0:T(8,128)S(1)}, u32[]{:S(2)}, u32[]{:S(2)}) collective-permute-start(f32[16,768]{1,0:T(8,128)S(1)} %add.146), channel_id=1, source_target_pairs={{0,2},{1,3},{2,0},{3,1},{4,5},{5,4},{6,7},{7,6},{8,10},{9,11},{10,... | collective-permute-start | bytes 147464 | tf_op jit(solution)/shard_map/ppermute | solution.py:586
  249.4 5.2 %collective-permute-start.51 = (bf16[96,768]{1,0:T(8,128)(2,1)S(1)}, bf16[96,768]{1,0:T(8,128)(2,1)S(1)}, u32[]{:S(2)}, u32[]{:S(2)}) collective-permute-start(bf16[96,768]{1,0:T(8,128)(2,1)S(1)} %fusion.27.refs_0_), channel_id=1, source_target_pairs={{0,8},{1,9},{2,10},{3,11},{4,20},{5,21},{6,22},{7,23},{8,0},{9,1},... | collective-permute-start | bytes 442376 | tf_op jit(solution)/shard_map/ppermute | solution.py:586
  254.6 6.8 %collective-permute-start.53 = (bf16[2,96,768]{2,1,0:T(8,128)(2,1)S(1)}, bf16[2,96,768]{2,1,0:T(8,128)(2,1)S(1)}, u32[]{:S(2)}, u32[]{:S(2)}) collective-permute-start(bf16[2,96,768]{2,1,0:T(8,128)(2,1)S(1)} %pad_maximum_fusion.13), channel_id=1, source_target_pairs={{0,16},{1,17},{2,18},{3,19},{4,12},{5,13},{6,14},{7,15},{8,24},{9,... | collective-permute-start | bytes 884744 | tf_op jit(solution)/shard_map/ppermute | solution.py:586
  261.4 4.0 %collective-permute-start.56 = (bf16[2,96,768]{2,1,0:T(8,128)(2,1)S(1)}, bf16[2,96,768]{2,1,0:T(8,128)(2,1)S(1)}, u32[]{:S(2)}, u32[]{:S(2)}) collective-permute-start(bf16[2,96,768]{2,1,0:T(8,128)(2,1)S(1)} %collective-permute-done.53.refs_2_), channel_id=1, source_target_pairs={{0,4},{1,5},{2,6},{3,7},{4,0},{5,1},{6,2},{7,3},{8,12},{9,13},{10,... | collective-permute-start | bytes 884744 | tf_op jit(solution)/shard_map/ppermute | solution.py:586
  263.5 1.8 collective-permute-start.54
  264.1 1.4 collective-permute-start.55
  (28 other events, 195.7 us)
